TPU v7x, 32 devices: a whole 2x2x4 slice. The times are simulated.
32 devices in a mesh: beam: 8 (over y, x, core), freq: 4 (over z).
Axes of the slice: x: 2, y: 2, z: 4, core: 2. Of those that a mesh axis runs over, the one named last changes fastest.
Arguments:
- intensity: bfloat16 [8, 16384, 256], P(None, ('freq', 'beam')), may hold values from -600 to 600, as said below
- channel_mask: int32 [16384], P('freq'), may hold values 0 or 1
- box_widths: int32 [9], replicated, may hold values from 1 to 64
Outputs:
- snr_peak: float32 [8, 4096], P('beam', 'freq')
Inputs may be any that keep to these rules, and one draw needn't show every extreme that they name: `intensity`: filterbank intensities of every beam and channel, of any sign.
All inputs are finite; a program needn't handle non-finite values. No bound on the sum of `channel_mask` on one device may be relied on, other than what follows from the above.
Results may differ from a plain program's by a relative error of at most 0.002.
Values may be sent and summed in bfloat16 or wider, within the bound.
A program may use at most 64 MiB of HBM per device.

v0:
```python
import jax
import jax.numpy as jnp
from jax import lax
from jax.experimental import pallas as pl
from jax.experimental.pallas import tpu as pltpu
from jax.sharding import PartitionSpec as P

CHANS = 16384
NDM = 4096
LANE_ROWS = 8
LANES = 128
WIDEST = 64

epsilon = 1e-05


def reverse_bits(number, count):
    result = 0
    for _ in range(count):
        result = result << 1 | number & 1
        number >>= 1
    return result


def lane_index(shape):
    return lax.broadcasted_iota(jnp.int32, shape, len(shape) - 1)


def earlier(block, amount):
    if amount == 0:
        return block
    samples = block.shape[-1]
    return jnp.where(lane_index(block.shape) < samples - amount, pltpu.roll(block, samples - amount, 1), 0.0)


def folds(trial_dev, samples):
    return trial_dev >= 4 * samples


def channel_limits(trial_dev, blocks, samples):
    limits = []
    for block in range(blocks):
        limit, rows = CHANS, NDM
        while (block * trial_dev * rows // NDM + 1) // 2 >= samples:
            limit, rows = limit // 2, rows // 2
        limits.append(limit)
    return limits


def entry_kernel(x_hbm, mask_ref, out_ref, x_ref, in_sem, send, send_sem, recv_sem, own_sem):
    blocks, beams, bands, samples = send.shape
    groups = lax.axis_size("beam")
    beam_dev = beams // groups
    width = x_ref.shape[1]
    group = width // (bands * blocks)
    trial_dev = NDM // blocks
    row_total = float(beams * samples)
    fold = folds(trial_dev, samples)
    limits = channel_limits(trial_dev, blocks, samples)
    my_block = lax.axis_index("freq")
    my_group = lax.axis_index("beam")
    my_place = my_block * groups + my_group
    devices = blocks * groups

    barrier = pltpu.get_barrier_semaphore()
    for step in range(1, devices):
        peer = (my_place + step) % devices
        pl.semaphore_signal(
            barrier, inc=1, device_id={"freq": peer // groups, "beam": peer % groups},
            device_id_type=pl.DeviceIdType.MESH,
        )

    chunks = in_sem.shape[0]
    span = width // chunks
    loads = [
        pltpu.make_async_copy(
            x_hbm.at[:, pl.ds(c * span, span)], x_ref.at[:, pl.ds(c * span, span)], in_sem.at[c]
        )
        for c in range(chunks)
    ]
    for load in loads:
        load.start()
    means, scales = [], []
    for c in range(chunks):
        loads[c].wait()
        total = jnp.zeros((span, samples), jnp.float32)
        squares = jnp.zeros((span, samples), jnp.float32)
        for beam in range(beams):
            wide = x_ref[beam, c * span:(c + 1) * span].astype(jnp.float32)
            total = total + wide
            squares = squares + wide * wide
        mean = jnp.sum(total, axis=1, keepdims=True) / row_total
        var = jnp.sum(squares, axis=1, keepdims=True) / row_total - mean * mean
        means.append(mean)
        scales.append(lax.rsqrt(var + epsilon))
    channel_mean = jnp.concatenate(means, axis=0)
    channel_scale = jnp.concatenate(scales, axis=0)
    out_row = lax.broadcasted_iota(jnp.int32, (blocks * bands, width), 0)
    channel = lax.broadcasted_iota(jnp.int32, (blocks * bands, width), 1)
    band = out_row % bands
    if fold:
        half = bands // 2
        band = (band % half) * 2 + band // half
    wanted = band * blocks + out_row // bands
    clean = mask_ref[:, pl.ds(pl.multiple_of(my_group * width, width), width)].astype(jnp.float32)
    chosen = jnp.where(channel // group == wanted, clean, 0.0).astype(jnp.bfloat16)
    upper = my_block * 2 >= blocks

    def message(block, slot, beam, rows):
        return pltpu.make_async_remote_copy(
            src_ref=send.at[block, slot, pl.ds(0, rows)],
            dst_ref=out_ref.at[beam % beam_dev, my_place, pl.ds(0, rows)],
            send_sem=send_sem.at[block, slot],
            recv_sem=recv_sem.at[beam % beam_dev, my_place],
            device_id={"freq": block, "beam": beam // beam_dev},
            device_id_type=pl.DeviceIdType.MESH,
        )

    def own_copy(slot, part):
        return pltpu.make_async_copy(
            send.at[my_block, slot], out_ref.at[part, my_place], own_sem.at[part]
        )

    def every_message(action, slot):
        beam = (my_group * beam_dev + slot) % beams
        for block in range(blocks):
            goes = my_place * width < limits[block]
            if slot < beam_dev:
                goes = goes & (my_block != block)
            if fold:
                @pl.when(goes & upper)
                def _(block=block):
                    action(message(block, slot, beam, bands // 2))
                goes = goes & jnp.logical_not(upper)

            @pl.when(goes)
            def _(block=block):
                action(message(block, slot, beam, bands))

    for slot in range(beams):
        beam = (my_group * beam_dev + slot) % beams
        wide = x_ref[beam].astype(jnp.float32)
        normed = ((wide - channel_mean) * channel_scale).astype(jnp.bfloat16)
        sums = jnp.dot(chosen, normed, preferred_element_type=jnp.float32)
        tree = [[sums[i * bands:(i + 1) * bands]] for i in range(blocks)]
        while len(tree) > 1:
            merged = []
            for low, high in zip(tree[0::2], tree[1::2]):
                merged.append(
                    [low[m // 2] + earlier(high[m // 2], (m + 1) // 2) for m in range(2 * len(low))]
                )
            tree = merged
        for number, row in enumerate(tree[0]):
            if fold:
                both = row[:half] + row[half:]
                row = jnp.concatenate([jnp.where(upper, both, row[:half]), row[half:]], axis=0)
            send[number, slot] = row.astype(jnp.bfloat16)
        if slot == 0:
            pl.semaphore_wait(barrier, devices - 1)
        every_message(lambda copy: copy.start(), slot)
        if slot < beam_dev:
            own_copy(slot, slot).start()

    for slot in range(beam_dev):
        own_copy(slot, slot).wait()
    limit = sum(jnp.where(my_block == block, limits[block], 0) for block in range(blocks))
    for place in range(devices):
        for part in range(beam_dev):
            rows = bands // 2 if fold and 2 * place >= devices else bands
            target = out_ref.at[part, place, pl.ds(0, rows)]
            @pl.when((place * width < limit) & (place != my_place))
            def _(target=target, place=place, part=part):
                pltpu.make_async_remote_copy(
                    src_ref=target, dst_ref=target, send_sem=send_sem.at[0, 0],
                    recv_sem=recv_sem.at[part, place],
                    device_id={"freq": my_block, "beam": my_group},
                    device_id_type=pl.DeviceIdType.MESH,
                ).wait_recv()
    for slot in range(beams):
        every_message(lambda copy: copy.wait_send(), slot)


def entry_rows(intensity, channel_mask):
    beams, width, samples = intensity.shape
    blocks, groups = lax.axis_size("freq"), lax.axis_size("beam")
    bands = width * NDM // (CHANS * blocks)
    beam_dev, devices = beams // groups, blocks * groups
    return pl.pallas_call(
        entry_kernel,
        in_specs=[pl.BlockSpec(memory_space=pl.ANY), pl.BlockSpec(memory_space=pltpu.VMEM)],
        out_specs=pl.BlockSpec(memory_space=pl.ANY),
        scratch_shapes=[
            pltpu.VMEM((beams, width, samples), jnp.bfloat16),
            pltpu.SemaphoreType.DMA((4,)),
            pltpu.VMEM((blocks, beams, bands, samples), jnp.bfloat16),
            pltpu.SemaphoreType.DMA((blocks, beams)),
            pltpu.SemaphoreType.DMA((beam_dev, devices)),
            pltpu.SemaphoreType.DMA((beam_dev,)),
        ],
        out_shape=jax.ShapeDtypeStruct((beam_dev, devices, bands, samples), jnp.bfloat16),
        compiler_params=pltpu.CompilerParams(collective_id=0, has_side_effects=True),
    )(intensity, channel_mask.reshape(1, -1))


def advanced(pieces, amount):
    lanes = pieces[0].shape[-1]
    position = lane_index(pieces[0].shape)
    turn = (lanes - amount) & (lanes - 1)
    turned = [pltpu.roll(piece, turn, 1) for piece in pieces]
    return joined(turned, lambda limit: position < limit - amount)


def advanced_rows(pieces, amounts):
    lanes = pieces[0].shape[-1]
    position = lane_index(pieces[0].shape) + amounts
    picks = position & (lanes - 1)
    turned = [jnp.take_along_axis(piece, picks, axis=1, mode="promise_in_bounds") for piece in pieces]
    return joined(turned, lambda limit: position < limit)


def joined(turned, below):
    lanes = turned[0].shape[-1]
    near = [below((k + 1) * lanes) for k in range(len(turned))]
    result = []
    for number in range(len(turned)):
        value = jnp.zeros_like(turned[0])
        for ahead in reversed(range(len(turned) - number)):
            value = jnp.where(near[ahead], turned[number + ahead], value)
        result.append(value)
    return result


def trial_kernel(place_ref, widths_ref, x_ref, out_ref, first, even, odd, series, prefix):
    total, samples = out_ref.shape[2], x_ref.shape[3]
    tiles = total // LANE_ROWS
    tile_bits = tiles.bit_length() - 1
    lanes = prefix.shape[2]
    parts = samples // lanes
    pitch = first.shape[1] // LANE_ROWS
    block = place_ref[0]
    bands = x_ref.shape[2]
    fold = folds(total, samples)
    half_bands = bands // 2
    sources = x_ref.shape[1]
    for number in range(sources):
        high, start = divmod(number * bands, tiles)
        start += reverse_bits(high, LANE_ROWS.bit_length() - 1) * pitch
        for part in range(parts):
            cut = slice(part * lanes, (part + 1) * lanes)
            if fold and 2 * number >= sources:
                first[part, start:start + half_bands] = x_ref[0, number, :half_bands, cut].astype(jnp.float32)
                first[part, start + half_bands:start + bands] = jnp.zeros((half_bands, lanes), jnp.float32)
            else:
                first[part, start:start + bands] = x_ref[0, number, :, cut].astype(jnp.float32)
    for tile in range(tiles):
        spot = tile
        if fold:
            band = tile % bands
            spot = tile - band + (band % 2) * half_bands + band // 2
        for part in range(parts):
            even[reverse_bits(tile, tile_bits), :, part * lanes:(part + 1) * lanes] = first[
                part, pl.ds(spot, LANE_ROWS, stride=pitch)
            ]

    source, target = even, odd
    count = 1
    while count < tiles:
        half = tiles // count // 2

        def merge(j, source=source, target=target, count=count, half=half):
            flat = (half * LANE_ROWS, lanes)
            cut = [slice(part * lanes, (part + 1) * lanes) for part in range(parts)]
            low = [source[pl.ds(j * 2 * half, half), :, c].reshape(flat) for c in cut]
            high = [source[pl.ds(j * 2 * half + half, half), :, c].reshape(flat) for c in cut]
            for side in range(2):
                moved = advanced(high, block * count + j + side)
                for c, base, extra in zip(cut, low, moved):
                    target[pl.ds((2 * j + side) * half, half), :, c] = (base + extra).reshape(
                        half, LANE_ROWS, lanes
                    )

        if count <= 16:
            for j in range(count):
                merge(j)
        else:
            def step(i, carry, merge=merge):
                for k in range(32):
                    merge(i * 32 + k)
                return carry
            lax.fori_loop(0, count // 32, step, 0)
        source, target = target, source
        count = count * 2

    spot = lax.broadcasted_iota(jnp.int32, (LANE_ROWS, lanes), 0)
    bits = [spot >> 2 & 1, spot >> 1 & 1, spot & 1]
    clear = [bit == 0 for bit in bits]

    def final_rows(j):
        pieces = [source[j, :, part * lanes:(part + 1) * lanes] for part in range(parts)]
        row = spot * 0 + (block * tiles + j)
        for level, reach in enumerate((4, 2, 1)):
            low, high = [], []
            for piece in pieces:
                down = pltpu.roll(piece, reach, 0)
                up = down if 2 * reach == LANE_ROWS else pltpu.roll(piece, LANE_ROWS - reach, 0)
                low.append(jnp.where(clear[level], piece, down))
                high.append(jnp.where(clear[level], up, piece))
            moved = advanced_rows(high, row + bits[level])
            pieces = [base + extra for base, extra in zip(low, moved)]
            row = 2 * row + bits[level]
        return jnp.concatenate(pieces, axis=1)

    def finish(i, carry):
        for k in range(16):
            pair = i * 16 + k
            rows = jnp.concatenate([final_rows(2 * pair), final_rows(2 * pair + 1)], axis=0)
            coarse = rows.astype(jnp.bfloat16)
            place = pl.ds(pl.multiple_of(pair * 16, 16), 16)
            series[place, :samples] = coarse
            series[place, samples:] = (rows - coarse.astype(jnp.float32)).astype(jnp.bfloat16)
        return carry

    lax.fori_loop(0, tiles // 32, finish, 0)

    until = lax.broadcasted_iota(jnp.int32, (samples, 2 * samples), 0)
    time = lax.broadcasted_iota(jnp.int32, (samples, 2 * samples), 1) & (samples - 1)
    ladder = jnp.where(time <= until, 1.0, 0.0).astype(jnp.bfloat16)
    margin = prefix.shape[1] - samples - LANE_ROWS
    piece = 2 * lanes
    for part in range(total // piece):
        sums = lax.dot_general(
            ladder, series[part * piece:(part + 1) * piece], (((1,), (1,)), ((), ())),
            preferred_element_type=jnp.float32,
        )
        for side in range(2):
            column = 2 * part + side
            prefix[column, :LANE_ROWS] = jnp.zeros((LANE_ROWS, lanes), jnp.float32)
            prefix[column, LANE_ROWS:LANE_ROWS + samples] = sums[:, side * lanes:(side + 1) * lanes]
            prefix[column, LANE_ROWS + samples:] = jnp.full((margin, lanes), -jnp.inf, jnp.float32)
    for column in range(total // lanes):
        best = None
        for number in range(widths_ref.shape[0]):
            width = widths_ref[number]
            sums = (
                prefix[column, pl.ds(LANE_ROWS - 1 + width, samples)]
                - prefix[column, LANE_ROWS - 1:LANE_ROWS - 1 + samples]
            )
            norm = lax.rsqrt(jnp.full((1, lanes), width * CHANS, jnp.int32).astype(jnp.float32))
            peak = jnp.max(sums, axis=0, keepdims=True) * norm
            best = peak if best is None else jnp.maximum(best, peak)
        out_ref[0, :, column * lanes:(column + 1) * lanes] = best


def trial_peaks(rows, box_widths, place):
    beams, devices, bands, samples = rows.shape
    total = devices * bands
    tiles = total // LANE_ROWS
    return pl.pallas_call(
        trial_kernel,
        grid_spec=pltpu.PrefetchScalarGridSpec(
            num_scalar_prefetch=2,
            grid=(beams,),
            in_specs=[pl.BlockSpec((1, devices, bands, samples), lambda b, p, w: (b, 0, 0, 0))],
            out_specs=pl.BlockSpec((1, 1, total), lambda b, p, w: (b, 0, 0)),
            scratch_shapes=[
                pltpu.VMEM((samples // LANES, total + LANE_ROWS * LANE_ROWS, LANES), jnp.float32),
                pltpu.VMEM((tiles, LANE_ROWS, samples), jnp.float32),
                pltpu.VMEM((tiles, LANE_ROWS, samples), jnp.float32),
                pltpu.VMEM((total, 2 * samples), jnp.bfloat16),
                pltpu.VMEM((total // LANES, LANE_ROWS + samples + WIDEST, LANES), jnp.float32),
            ],
        ),
        out_shape=jax.ShapeDtypeStruct((beams, 1, total), jnp.float32),
    )(place, box_widths, rows)[:, 0]


def shards(intensity, channel_mask, box_widths):
    rows = entry_rows(intensity, channel_mask)
    return trial_peaks(rows, box_widths, lax.axis_index("freq").reshape(1))


def solution(mesh):
    in_specs = (P(None, ("freq", "beam"), None), P("freq"), P())
    out_specs = P("beam", "freq")
    return jax.shard_map(shards, mesh=mesh, in_specs=in_specs, out_specs=out_specs, check_vma=False)
```

profile of v0, /device:TPU:0, one launch (start us, length us, event | category | flops | bytes accessed | tf_op | source)
XLA Modules:
  0.0 29.5 jit_solution(597220869878629304)
XLA Ops:
  0.0 17.2 %shard_map.37.x_ref = bf16[1,32,32,256]{3,2,1,0:T(8,128)(2,1)} custom-call(bf16[8,512,256]{2,1,0:T(8,128)(2,1)} %x_hbm.1, s32[1,4096]{1,0:T(1,128)} %bitcast.3), custom_call_target="tpu_custom_call" | custom-call | tf_op jit(solution)/shard_map/pallas_call | solution.py:188
  17.2 12.2 %shard_map.38 = f32[1,1,1024]{2,1,0:T(1,128)} custom-call(s32[1]{0:T(128)} %bitcast.place_ref, s32[9]{0:T(128)} %widths_ref.1, bf16[1,32,32,256]{3,2,1,0:T(8,128)(2,1)} %shard_map.37.x_ref), custom_call_target="tpu_custom_call" | custom-call | tf_op jit(solution)/shard_map/pallas_call | solution.py:358
where the time goes:
time: 29.7 us; the launch traced here: 29.5 us
  Pallas kernels  29.4 us (99%)
    pallas_call x1, Pallas kernels, entry_rows(): pl.pallas_call(entry_kernel, in_specs=[pl.BlockSpec(memory_space=pl.ANY),...  17.2 us
    pallas_call x1, Pallas kernels, trial_peaks(): pl.pallas_call(trial_kernel, grid_spec=pltpu.PrefetchScalarGridSpec(num_s...  12.2 us

commit v1 on v0

--- a/solution.py
+++ b/solution.py
@@ -374,7 +374,524 @@
     )(place, box_widths, rows)[:, 0]
 
 
+def compact(samples, devices, blocks, groups, beams, width):
+    return (
+        samples == 2 * LANES and NDM == 16 * samples and blocks == 4 and beams == groups
+        and devices * LANE_ROWS == samples and width * devices == CHANS
+    )
+
+
+LAYERS = (3, 2, 1, 0)
+ORDER = (0, 2, 1, 3)
+
+
+def device_kind(block, group, groups):
+    lower = jnp.where(group * 2 < groups, 0, 1)
+    return jnp.where(block == 0, lower, jnp.where(block == 1, 2, 3))
+
+
+def kind_span(kind):
+    return ((0, 8), (0, 8), (2, 8), (3, 6))[kind]
+
+
+def late_span(place, whole):
+    return (0, 8) if place < whole else (4, 8)
+
+
+def band_mask(kind, width):
+    depth = LAYERS[kind]
+    rows = LANE_ROWS * (2 << depth)
+    row = lax.broadcasted_iota(jnp.int32, (rows, width), 0)
+    channel = lax.broadcasted_iota(jnp.int32, (rows, width), 1)
+    inner, tile = row % LANE_ROWS, row // LANE_ROWS
+    if kind == 3:
+        wanted = inner * 2 + tile
+    else:
+        quarter = tile % 4
+        band = inner * 4 + (quarter % 2) * 2 + quarter // 2
+        wanted = band * (rows // (4 * LANE_ROWS)) + tile // 4
+    return channel // (width * LANE_ROWS // (rows * LANE_ROWS)) == wanted
+
+
+def stepped(pair, amount):
+    if amount == 0:
+        return list(pair)
+    lane = lane_index(pair[0].shape)
+    near = lane < LANES - amount
+    turned = [pltpu.roll(piece, LANES - amount, 1) for piece in pair]
+    return [jnp.where(near, turned[0], turned[1]), jnp.where(near, turned[1], 0.0)]
+
+
+def plus(low, high):
+    return [a + b for a, b in zip(low, high)]
+
+
+def leaf_rows(kind, tiles):
+    if kind == 3:
+        wide = tiles
+    else:
+        per = len(tiles) // 4
+        quarters = [tiles[q] for q in range(4)]
+        parts = [[tiles[u * 4 + q] for q in range(4)] for u in range(per)]
+        if per == 4:
+            one = [plus(parts[0][q], stepped(parts[1][q], 1)) for q in range(4)]
+            two = [plus(parts[2][q], stepped(parts[3][q], 1)) for q in range(4)]
+            halves = [
+                [plus(parts[0][q], parts[1][q]) for q in range(4)],
+                [plus(parts[2][q], parts[3][q]) for q in range(4)],
+            ]
+        elif per == 2:
+            halves = parts
+        if per >= 2:
+            quarters = [plus(halves[0][q], halves[1][q]) for q in range(4)]
+        wide = [plus(quarters[0], quarters[2]), plus(quarters[1], quarters[3])]
+    zero = plus(wide[0], wide[1])
+    first = plus(wide[0], stepped(wide[1], 1))
+    message = [None, None, first[0], first[1], zero[0], zero[1], None, None]
+    out = {0: message}
+    if kind != 3:
+        second = [plus(quarters[a], stepped(quarters[2 + a], 1)) for a in range(2)]
+        message[0], message[1] = second[0][0], second[1][0]
+        message[6], message[7] = second[0][1], second[1][1]
+        if per >= 2:
+            third = [plus(halves[0][q], stepped(halves[1][q], 1)) for q in range(4)]
+            out[1] = [tile[0] for tile in third] + [tile[1] for tile in third]
+        if per == 4:
+            for block in (2, 3):
+                fourth = [plus(one[q], stepped(two[q], block - 1)) for q in range(4)]
+                out[block] = [tile[0] for tile in fourth] + [tile[1] for tile in fourth]
+    return out
+
+
+def spread_kernel(x_hbm, mask_ref, out_ref, x_ref, in_sem, send, send_sem, recv_sem, own_sem):
+    beams, width, samples = x_ref.shape
+    blocks, groups = lax.axis_size("freq"), lax.axis_size("beam")
+    devices = blocks * groups
+    row_total = float(beams * samples)
+    my_block = lax.axis_index("freq")
+    my_group = lax.axis_index("beam")
+    my_place = my_block * groups + my_group
+    kind_here = device_kind(my_block, my_group, groups)
+    sources = (devices, groups, groups // 2, groups // 2)
+
+    chunks = in_sem.shape[0]
+    span = width // chunks
+    loads = [
+        pltpu.make_async_copy(
+            x_hbm.at[:, pl.ds(c * span, span)], x_ref.at[:, pl.ds(c * span, span)], in_sem.at[c]
+        )
+        for c in range(chunks)
+    ]
+    for load in loads:
+        load.start()
+
+    barrier = pltpu.get_barrier_semaphore()
+    for block in range(blocks):
+        @pl.when(my_block == block)
+        def _(block=block):
+            for step in range(1, devices):
+                place = (my_place + step) % devices
+                if sources[block] == devices:
+                    pl.semaphore_signal(
+                        barrier, inc=1, device_id={"freq": place // groups, "beam": place % groups},
+                        device_id_type=pl.DeviceIdType.MESH,
+                    )
+            if sources[block] < devices:
+                for place in range(sources[block]):
+                    pl.semaphore_signal(
+                        barrier, inc=1, device_id={"freq": place // groups, "beam": place % groups},
+                        device_id_type=pl.DeviceIdType.MESH,
+                    )
+
+    lane = lax.broadcasted_iota(jnp.int32, (LANE_ROWS, LANES), 1)
+    inner = lax.broadcasted_iota(jnp.int32, (LANE_ROWS, LANES), 0)
+    ones = jnp.ones((2 * LANE_ROWS, samples), jnp.bfloat16)
+    dims = (((1,), (1,)), ((), ()))
+    means, scales = [], []
+    for c in range(chunks):
+        loads[c].wait()
+        rows = slice(c * span, (c + 1) * span)
+        dotted = beams // 2
+        flat = jnp.concatenate([x_ref[b, rows] for b in range(dotted)], axis=1)
+        rest = jnp.concatenate([x_ref[b, rows] for b in range(dotted, beams)], axis=1)
+        gram = lax.dot_general(flat, flat, dims, preferred_element_type=jnp.float32)
+        total = lax.dot_general(
+            jnp.concatenate([ones] * beams, axis=1), jnp.concatenate([flat, rest], axis=1), dims,
+            preferred_element_type=jnp.float32,
+        )[:1]
+        squares = []
+        for column in range(span // LANES):
+            sums = jnp.zeros((LANE_ROWS, LANES), jnp.float32)
+            for tile in range(LANES // LANE_ROWS):
+                at = column * LANES + tile * LANE_ROWS
+                own = jnp.zeros((LANE_ROWS, samples), jnp.float32)
+                for b in range(dotted, beams):
+                    wide = x_ref[b, c * span + at:c * span + at + LANE_ROWS].astype(jnp.float32)
+                    own = own + wide * wide
+                own = jnp.sum(own, axis=1, keepdims=True)
+                both = gram[at:at + LANE_ROWS, column * LANES:(column + 1) * LANES] + own
+                sums = sums + jnp.where(lane == inner + tile * LANE_ROWS, both, 0.0)
+            squares.append(jnp.sum(sums, axis=0, keepdims=True))
+        mean = total / row_total
+        var = jnp.concatenate(squares, axis=1) / row_total - mean * mean
+        place = pl.multiple_of(my_group * width + c * span, span)
+        clean = mask_ref[:, pl.ds(place, span)].astype(jnp.float32)
+        means.append(mean)
+        scales.append(lax.rsqrt(var + epsilon) * clean)
+    channel_mean = jnp.concatenate(means, axis=1)
+    channel_scale = jnp.concatenate(scales, axis=1)
+    coarse = channel_scale.astype(jnp.bfloat16).astype(jnp.float32)
+    fine = (channel_scale - coarse).astype(jnp.bfloat16).astype(jnp.float32)
+    offset = channel_mean * (coarse + fine)
+
+    def message(block, slot, first, last):
+        beam = (my_group + slot) % beams
+        return pltpu.make_async_remote_copy(
+            src_ref=send.at[block, slot, pl.ds(first, last - first)],
+            dst_ref=out_ref.at[0, my_place, pl.ds(first, last - first)],
+            send_sem=send_sem.at[block, slot],
+            recv_sem=recv_sem.at[my_place],
+            device_id={"freq": block, "beam": beam},
+            device_id_type=pl.DeviceIdType.MESH,
+        )
+
+    def own_copy():
+        return pltpu.make_async_copy(send.at[0, 0], out_ref.at[0, my_place], own_sem.at[0])
+
+    def outgoing(action, kind, slot):
+        if kind < 2 and slot == 0:
+            pass
+        else:
+            action(message(0, slot, *kind_span(kind)))
+        if kind == 0:
+            action(message(1, slot, 0, 8))
+            for half in range(2):
+                @pl.when((my_group * 4 >= groups) if half else (my_group * 4 < groups))
+                def _(half=half):
+                    for block in (2, 3):
+                        action(message(block, slot, 4 * half, 8))
+        if kind == 1:
+            action(message(1, slot, 4, 8))
+
+    targets = (devices - 1, 2 * groups - 1, groups, groups)
+    for kind in range(4):
+        @pl.when(kind_here == kind)
+        def _(kind=kind):
+            chosen = band_mask(kind, width)
+            rows = chosen.shape[0]
+            matrix = jnp.concatenate(
+                [jnp.where(chosen, coarse, 0.0), jnp.where(chosen, fine, 0.0)], axis=0
+            ).astype(jnp.bfloat16)
+            shift = jnp.sum(jnp.where(chosen, offset, 0.0), axis=1, keepdims=True)
+            for slot in range(beams):
+                beam = (my_group + slot) % beams
+                both = jnp.dot(matrix, x_ref[beam], preferred_element_type=jnp.float32)
+                sums = both[:rows] + both[rows:] - shift
+                tiles = [
+                    [sums[t * LANE_ROWS:(t + 1) * LANE_ROWS, p * LANES:(p + 1) * LANES] for p in range(2)]
+                    for t in range(rows // LANE_ROWS)
+                ]
+                for block, leaves in leaf_rows(kind, tiles).items():
+                    for number, leaf in enumerate(leaves):
+                        if leaf is not None:
+                            send[block, slot, number] = leaf.astype(jnp.bfloat16)
+                if slot == 0:
+                    pl.semaphore_wait(barrier, targets[kind])
+                outgoing(lambda copy: copy.start(), kind, slot)
+                if kind < 2 and slot == 0:
+                    own_copy().start()
+
+    def arrival(place, first, last):
+        target = out_ref.at[0, place, pl.ds(first, last - first)]
+        pltpu.make_async_remote_copy(
+            src_ref=target, dst_ref=target, send_sem=send_sem.at[0, 0], recv_sem=recv_sem.at[place],
+            device_id={"freq": my_block, "beam": my_group}, device_id_type=pl.DeviceIdType.MESH,
+        ).wait_recv()
+
+    @pl.when(my_block == 0)
+    def _():
+        own_copy().wait()
+        for place in range(devices):
+            kind = max(place // groups, 0)
+            extent = kind_span(0 if kind == 0 else min(kind + 1, 3))
+
+            @pl.when(place != my_place)
+            def _(place=place, extent=extent):
+                arrival(place, *extent)
+
+    @pl.when(my_block == 1)
+    def _():
+        for place in range(groups):
+            arrival(place, *late_span(place, groups // 2))
+
+    @pl.when(my_block > 1)
+    def _():
+        for place in range(groups // 2):
+            arrival(place, *late_span(place, groups // 4))
+
+    for kind in range(4):
+        @pl.when(kind_here == kind)
+        def _(kind=kind):
+            for slot in range(beams):
+                outgoing(lambda copy: copy.wait_send(), kind, slot)
+
+
+def spread_rows(intensity, channel_mask):
+    beams, width, samples = intensity.shape
+    blocks, groups = lax.axis_size("freq"), lax.axis_size("beam")
+    devices = blocks * groups
+    return pl.pallas_call(
+        spread_kernel,
+        in_specs=[pl.BlockSpec(memory_space=pl.ANY), pl.BlockSpec(memory_space=pltpu.VMEM)],
+        out_specs=pl.BlockSpec(memory_space=pl.ANY),
+        scratch_shapes=[
+            pltpu.VMEM((beams, width, samples), jnp.bfloat16),
+            pltpu.SemaphoreType.DMA((2,)),
+            pltpu.VMEM((blocks, beams, 8, LANE_ROWS, LANES), jnp.bfloat16),
+            pltpu.SemaphoreType.DMA((blocks, beams)),
+            pltpu.SemaphoreType.DMA((devices,)),
+            pltpu.SemaphoreType.DMA((1,)),
+        ],
+        out_shape=jax.ShapeDtypeStruct((1, devices, 8, LANE_ROWS, LANES), jnp.bfloat16),
+        compiler_params=pltpu.CompilerParams(collective_id=0, has_side_effects=True),
+    )(intensity, channel_mask.reshape(1, -1))
+
+
+def ramped(pair, start, stride, far, only_late=False):
+    shape = pair[1].shape
+    place = lane_index(shape) + (lax.broadcasted_iota(jnp.int32, shape, 0) * stride + start)
+    picks = place & (LANES - 1)
+    late = jnp.take_along_axis(pair[1], picks, axis=1, mode="promise_in_bounds")
+    if far:
+        return [jnp.where(place < 2 * LANES, late, 0.0), None]
+    near = place < LANES
+    moved = [None, jnp.where(near, late, 0.0)]
+    if not only_late:
+        early = jnp.take_along_axis(pair[0], picks, axis=1, mode="promise_in_bounds")
+        moved[0] = jnp.where(near, early, late)
+    return moved
+
+
+def joined_pair(low, high):
+    return [a if b is None else (None if a is None else a + b) for a, b in zip(low, high)]
+
+
+def unit_rows(x_ref, first, work, mid, series, base, root, leaves, kinds, found):
+    tiles = leaves // LANE_ROWS
+    pitch = first.shape[1] // LANE_ROWS
+    for address, place, numbers in found:
+        for part in range(2):
+            if numbers[part] is not None:
+                first[part, address:address + LANE_ROWS] = x_ref[0, place, numbers[part]].astype(jnp.float32)
+
+    def leaf(tile, part):
+        outer, kind = tile >> kinds, tile & ((1 << kinds) - 1)
+        if leaves == LANE_ROWS * (pitch - LANE_ROWS):
+            spot, step = ((outer >> 3 << kinds) + kind) * LANE_ROWS + (outer & 7), pitch
+        else:
+            spot, step = kind * pitch + outer, LANE_ROWS // 2
+        return first[part, pl.ds(spot, LANE_ROWS, stride=step)]
+
+    chunk = 8
+    for c in range(tiles // chunk):
+        tree = [[[leaf(c * chunk + k, part) for part in range(2)]] for k in range(chunk)]
+        level_root = root
+        while len(tree) > 1:
+            tree = [
+                [
+                    plus(low[r // 2], stepped(high[r // 2], level_root + r // 2 + r % 2))
+                    for r in range(2 * len(low))
+                ]
+                for low, high in zip(tree[0::2], tree[1::2])
+            ]
+            level_root = level_root * 2
+        for j in range(chunk):
+            for part in range(2):
+                at = (j * (tiles // chunk) + c) * LANE_ROWS
+                work[part, at:at + LANE_ROWS] = tree[0][j][part]
+    chunks = tiles // chunk
+    for j in range(chunk):
+        tree = []
+        for c in range(chunks):
+            at = (j * chunks + c) * LANE_ROWS
+            tree.append([[work[part, at:at + LANE_ROWS] for part in range(2)]])
+        level_root = root * chunk + j
+        while len(tree) > 1:
+            tree = [
+                [
+                    plus(low[r // 2], stepped(high[r // 2], level_root + r // 2 + r % 2))
+                    for r in range(2 * len(low))
+                ]
+                for low, high in zip(tree[0::2], tree[1::2])
+            ]
+            level_root = level_root * 2
+        for k in range(chunks):
+            for part in range(2):
+                at = (j * chunks + k) * LANE_ROWS
+                mid[part, at:at + LANE_ROWS] = tree[0][k][part]
+    far = root > 0
+    for g in range(tiles // LANE_ROWS):
+        tree = []
+        for s in range(LANE_ROWS):
+            pair = [
+                None if far and 2 * s >= LANE_ROWS and part == 0
+                else mid[part, pl.ds(g * LANE_ROWS * LANE_ROWS + s, LANE_ROWS, stride=LANE_ROWS)]
+                for part in range(2)
+            ]
+            tree.append([pair])
+        start, stride = root * tiles + g * LANE_ROWS, 1
+        while len(tree) > 1:
+            last = len(tree) == 2
+            merged = []
+            for number in range(len(tree) // 2):
+                low, high = tree[2 * number], tree[2 * number + 1]
+                rows = []
+                for r in range(2 * len(low)):
+                    source = r // 2
+                    begin = start + source + r % 2
+                    missing = high[source][0] is None
+                    moved = ramped(high[source], begin, stride, far and last, missing)
+                    rows.append(joined_pair(low[source], moved))
+                merged.append(rows)
+            tree = merged
+            start, stride = start * 2, stride * 2
+        for k in range(0, LANE_ROWS, 2):
+            rows = jnp.concatenate(
+                [jnp.concatenate(tree[0][k + half], axis=1) for half in range(2)], axis=0
+            )
+            coarse = rows.astype(jnp.bfloat16)
+            at = base + g * 64 + k * LANE_ROWS
+            samples = rows.shape[1]
+            series[at:at + 2 * LANE_ROWS, :samples] = coarse
+            series[at:at + 2 * LANE_ROWS, samples:] = (rows - coarse.astype(jnp.float32)).astype(jnp.bfloat16)
+
+
+def boxcar_rows(widths_ref, series, prefix, columns):
+    lanes = prefix.shape[2]
+    samples = series.shape[1] // 2
+    until = lax.broadcasted_iota(jnp.int32, (samples, 2 * samples), 0)
+    time = lax.broadcasted_iota(jnp.int32, (samples, 2 * samples), 1) & (samples - 1)
+    ladder = jnp.where(time <= until, 1.0, 0.0).astype(jnp.bfloat16)
+    margin = prefix.shape[1] - samples - LANE_ROWS
+    piece = min(2, columns)
+    for part in range(columns // piece):
+        sums = lax.dot_general(
+            ladder, series[part * piece * lanes:(part + 1) * piece * lanes], (((1,), (1,)), ((), ())),
+            preferred_element_type=jnp.float32,
+        )
+        for side in range(piece):
+            column = piece * part + side
+            prefix[column, :LANE_ROWS] = jnp.zeros((LANE_ROWS, lanes), jnp.float32)
+            prefix[column, LANE_ROWS:LANE_ROWS + samples] = sums[:, side * lanes:(side + 1) * lanes]
+            prefix[column, LANE_ROWS + samples:] = jnp.full((margin, lanes), -jnp.inf, jnp.float32)
+    result = []
+    for column in range(columns):
+        best = None
+        for number in range(widths_ref.shape[0]):
+            width = widths_ref[number]
+            sums = (
+                prefix[column, pl.ds(LANE_ROWS - 1 + width, samples)]
+                - prefix[column, LANE_ROWS - 1:LANE_ROWS - 1 + samples]
+            )
+            norm = lax.rsqrt(jnp.full((1, lanes), width * CHANS, jnp.int32).astype(jnp.float32))
+            peak = jnp.max(sums, axis=0, keepdims=True) * norm
+            best = peak if best is None else jnp.maximum(best, peak)
+        result.append(jnp.broadcast_to(best, (LANE_ROWS, lanes)))
+    return result
+
+
+def unpermuted(columns, out_ref, offset, repeat_bits):
+    lane = lane_index((LANE_ROWS, LANES))
+    for number in range(len(columns) << repeat_bits):
+        row = (lane + number * LANES) >> repeat_bits
+        row = row & (LANES - 1)
+        picks = (row & 64) + (row & 7) * LANE_ROWS + ((row >> 3) & 7)
+        column = columns[number >> repeat_bits]
+        spread = jnp.take_along_axis(column, picks, axis=1, mode="promise_in_bounds")
+        at = offset + number * LANES
+        out_ref[0, :, at:at + LANES] = spread[:1]
+
+
+def peaks_kernel(widths_ref, x_ref, out_ref, first, work, mid, series, prefix):
+    block = lax.axis_index("freq")
+    groups = lax.axis_size("beam")
+    pitch = first.shape[1] // LANE_ROWS
+    args = (x_ref, first, work, mid, series)
+
+    def wide_places(devices, numbers_of):
+        found = []
+        per = devices // LANE_ROWS
+        for place in range(devices):
+            s, b = divmod(place, per)
+            for address, numbers in numbers_of(place):
+                found.append((s * pitch + b * (pitch - LANE_ROWS) // per + address, place, numbers))
+        return found
+
+    @pl.when(block == 0)
+    def _():
+        unit_rows(*args, 512, 1, 256, 1, wide_places(
+            2 * groups,
+            lambda place: [(8 * a, (a if place < groups else None, 6 + a)) for a in range(2)],
+        ))
+        unit_rows(*args, 256, 1, 256, 0, wide_places(
+            4 * groups, lambda place: [(0, (2 if place < 2 * groups else None, 3))],
+        ))
+        unit_rows(*args, 0, 0, 256, 0, wide_places(4 * groups, lambda place: [(0, (4, 5))]))
+        result = boxcar_rows(widths_ref, series, prefix, 6)
+        unpermuted(result[:4], out_ref, 0, 0)
+        unpermuted(result[4:], out_ref, 512, 1)
+
+    @pl.when(block == 1)
+    def _():
+        unit_rows(*args, 0, 1, 256, 2, wide_places(
+            groups,
+            lambda place: [
+                (8 * (2 * (q % 2) + q // 2), (q if 2 * place < groups else None, 4 + q)) for q in range(4)
+            ],
+        ))
+        unpermuted(boxcar_rows(widths_ref, series, prefix, 2), out_ref, 0, 2)
+
+    for late in (2, 3):
+        @pl.when(block == late)
+        def _(late=late):
+            found = []
+            for place in range(groups // 2):
+                for q in range(4):
+                    found.append((
+                        (2 * (q % 2) + q // 2) * pitch + place * LANE_ROWS, place,
+                        (q if 4 * place < groups else None, 4 + q),
+                    ))
+            unit_rows(*args, 0, late, 128, 2, found)
+            unpermuted(boxcar_rows(widths_ref, series, prefix, 1), out_ref, 0, 3)
+
+
+def beam_peaks(rows, box_widths):
+    samples = 2 * LANES
+    total = 4 * samples
+    return pl.pallas_call(
+        peaks_kernel,
+        grid_spec=pltpu.PrefetchScalarGridSpec(
+            num_scalar_prefetch=1,
+            grid=(1,),
+            in_specs=[pl.BlockSpec(rows.shape, lambda b, w: (0, 0, 0, 0, 0))],
+            out_specs=pl.BlockSpec((1, 1, total), lambda b, w: (0, 0, 0)),
+            scratch_shapes=[
+                pltpu.VMEM((2, samples + LANE_ROWS * LANE_ROWS, LANES), jnp.float32),
+                pltpu.VMEM((2, samples, LANES), jnp.float32),
+                pltpu.VMEM((2, samples, LANES), jnp.float32),
+                pltpu.VMEM((3 * samples, 2 * samples), jnp.bfloat16),
+                pltpu.VMEM((6, LANE_ROWS + samples + WIDEST, LANES), jnp.float32),
+            ],
+        ),
+        out_shape=jax.ShapeDtypeStruct((1, 1, total), jnp.float32),
+    )(box_widths, rows)[:, 0]
+
+
 def shards(intensity, channel_mask, box_widths):
+    beams, width, samples = intensity.shape
+    blocks, groups = lax.axis_size("freq"), lax.axis_size("beam")
+    if compact(samples, blocks * groups, blocks, groups, beams, width):
+        return beam_peaks(spread_rows(intensity, channel_mask), box_widths)
     rows = entry_rows(intensity, channel_mask)
     return trial_peaks(rows, box_widths, lax.axis_index("freq").reshape(1))
 

time: 29.7 us -> 25.4 us (0.86)
  Pallas kernels: 29.4 us -> 25.1 us
    pallas_call x2, Pallas kernels: 29.4 us -> 25.1 us  [the longest x1 17.2 us: spread_rows(): pl.pallas_call(spread_kernel, in_specs=[pl.BlockSpec(memory_space=pl.ANY)...]
where the time goes in v1:
time: 25.4 us; the launch traced here: 25.2 us
  Pallas kernels  25.1 us (99%)
    pallas_call x1, Pallas kernels, spread_rows(): pl.pallas_call(spread_kernel, in_specs=[pl.BlockSpec(memory_space=pl.ANY)...  17.2 us
    pallas_call x1, Pallas kernels, beam_peaks(): pl.pallas_call(peaks_kernel, grid_spec=pltpu.PrefetchScalarGridSpec(num_s...  7.93 us

profile of v1, /device:TPU:0, one launch (start us, length us, event | category | flops | bytes accessed | tf_op | source)
XLA Modules:
  0.0 25.2 jit_solution(10776715674812902367)
XLA Ops:
  0.0 17.2 %shard_map.37.x_ref = bf16[1,32,8,8,128]{4,3,2,1,0:T(8,128)(2,1)} custom-call(bf16[8,512,256]{2,1,0:T(8,128)(2,1)} %x_hbm.1, s32[1,4096]{1,0:T(1,128)} %bitcast.2), custom_call_target="tpu_custom_call" | custom-call | tf_op jit(solution)/shard_map/pallas_call | solution.py:643
  17.2 7.9 %shard_map.38 = f32[1,1,1024]{2,1,0:T(1,128)} custom-call(s32[9]{0:T(128)} %widths_ref.1, bf16[1,32,8,8,128]{4,3,2,1,0:T(8,128)(2,1)} %shard_map.37.x_ref), custom_call_target="tpu_custom_call" | custom-call | tf_op jit(solution)/shard_map/pallas_call | solution.py:871

commit v2 on v1

--- a/solution.py
+++ b/solution.py
@@ -381,36 +381,26 @@
     )
 
 
-LAYERS = (3, 2, 1, 0)
-ORDER = (0, 2, 1, 3)
-
-
-def device_kind(block, group, groups):
-    lower = jnp.where(group * 2 < groups, 0, 1)
-    return jnp.where(block == 0, lower, jnp.where(block == 1, 2, 3))
-
-
-def kind_span(kind):
-    return ((0, 8), (0, 8), (2, 8), (3, 6))[kind]
+def block_span(block):
+    return ((0, 8), (2, 8), (3, 6), (3, 6))[block]
 
 
 def late_span(place, whole):
     return (0, 8) if place < whole else (4, 8)
 
 
-def band_mask(kind, width):
-    depth = LAYERS[kind]
+def band_mask(depth, width):
     rows = LANE_ROWS * (2 << depth)
     row = lax.broadcasted_iota(jnp.int32, (rows, width), 0)
     channel = lax.broadcasted_iota(jnp.int32, (rows, width), 1)
     inner, tile = row % LANE_ROWS, row // LANE_ROWS
-    if kind == 3:
+    if depth == 0:
         wanted = inner * 2 + tile
     else:
         quarter = tile % 4
         band = inner * 4 + (quarter % 2) * 2 + quarter // 2
         wanted = band * (rows // (4 * LANE_ROWS)) + tile // 4
-    return channel // (width * LANE_ROWS // (rows * LANE_ROWS)) == wanted
+    return channel // (width // rows) == wanted
 
 
 def stepped(pair, amount):
@@ -426,44 +416,36 @@
     return [a + b for a, b in zip(low, high)]
 
 
-def leaf_rows(kind, tiles):
-    if kind == 3:
+def near_leaves(tiles):
+    if len(tiles) == 4:
+        wide = [plus(tiles[0], tiles[2]), plus(tiles[1], tiles[3])]
+    else:
         wide = tiles
-    else:
-        per = len(tiles) // 4
-        quarters = [tiles[q] for q in range(4)]
-        parts = [[tiles[u * 4 + q] for q in range(4)] for u in range(per)]
-        if per == 4:
-            one = [plus(parts[0][q], stepped(parts[1][q], 1)) for q in range(4)]
-            two = [plus(parts[2][q], stepped(parts[3][q], 1)) for q in range(4)]
-            halves = [
-                [plus(parts[0][q], parts[1][q]) for q in range(4)],
-                [plus(parts[2][q], parts[3][q]) for q in range(4)],
-            ]
-        elif per == 2:
-            halves = parts
-        if per >= 2:
-            quarters = [plus(halves[0][q], halves[1][q]) for q in range(4)]
-        wide = [plus(quarters[0], quarters[2]), plus(quarters[1], quarters[3])]
     zero = plus(wide[0], wide[1])
     first = plus(wide[0], stepped(wide[1], 1))
     message = [None, None, first[0], first[1], zero[0], zero[1], None, None]
-    out = {0: message}
-    if kind != 3:
-        second = [plus(quarters[a], stepped(quarters[2 + a], 1)) for a in range(2)]
+    if len(tiles) == 4:
+        second = [plus(tiles[a], stepped(tiles[2 + a], 1)) for a in range(2)]
         message[0], message[1] = second[0][0], second[1][0]
         message[6], message[7] = second[0][1], second[1][1]
-        if per >= 2:
-            third = [plus(halves[0][q], stepped(halves[1][q], 1)) for q in range(4)]
-            out[1] = [tile[0] for tile in third] + [tile[1] for tile in third]
-        if per == 4:
-            for block in (2, 3):
-                fourth = [plus(one[q], stepped(two[q], block - 1)) for q in range(4)]
-                out[block] = [tile[0] for tile in fourth] + [tile[1] for tile in fourth]
-    return out
-
-
-def spread_kernel(x_hbm, mask_ref, out_ref, x_ref, in_sem, send, send_sem, recv_sem, own_sem):
+    return message
+
+
+def far_leaves(tiles):
+    parts = [tiles[at:at + 4] for at in range(0, len(tiles), 4)]
+    halves = parts if len(parts) == 2 else [[plus(a, b) for a, b in zip(*parts[at:at + 2])] for at in (0, 2)]
+    out = {1: [plus(low, stepped(high, 1)) for low, high in zip(*halves)]}
+    if len(parts) == 4:
+        one, two = [[plus(a, stepped(b, 1)) for a, b in zip(*parts[at:at + 2])] for at in (0, 2)]
+        for block in (2, 3):
+            out[block] = [plus(low, stepped(high, block - 1)) for low, high in zip(one, two)]
+    return {block: [pair[part] for part in range(2) for pair in pairs] for block, pairs in out.items()}
+
+
+def search_kernel(
+    x_hbm, mask_hbm, widths_hbm, out_ref, x_ref, mask_ref, widths_ref, in_sem, send, send_sem, recv, recv_sem,
+    ready_sem, first, work, mid, series, prefix,
+):
     beams, width, samples = x_ref.shape
     blocks, groups = lax.axis_size("freq"), lax.axis_size("beam")
     devices = blocks * groups
@@ -471,10 +453,9 @@
     my_block = lax.axis_index("freq")
     my_group = lax.axis_index("beam")
     my_place = my_block * groups + my_group
-    kind_here = device_kind(my_block, my_group, groups)
-    sources = (devices, groups, groups // 2, groups // 2)
-
-    chunks = in_sem.shape[0]
+    quarter = groups // 2
+
+    chunks = in_sem.shape[0] - 2
     span = width // chunks
     loads = [
         pltpu.make_async_copy(
@@ -482,26 +463,31 @@
         )
         for c in range(chunks)
     ]
-    for load in loads:
+    mask_load = pltpu.make_async_copy(mask_hbm, mask_ref, in_sem.at[chunks])
+    widths_load = pltpu.make_async_copy(widths_hbm, widths_ref, in_sem.at[chunks + 1])
+    loads[0].start()
+    mask_load.start()
+    for load in loads[1:]:
         load.start()
+    widths_load.start()
+
+    def signal(semaphore, place):
+        pl.semaphore_signal(
+            semaphore, inc=1, device_id={"freq": place // groups, "beam": place % groups},
+            device_id_type=pl.DeviceIdType.MESH,
+        )
 
     barrier = pltpu.get_barrier_semaphore()
-    for block in range(blocks):
-        @pl.when(my_block == block)
-        def _(block=block):
-            for step in range(1, devices):
-                place = (my_place + step) % devices
-                if sources[block] == devices:
-                    pl.semaphore_signal(
-                        barrier, inc=1, device_id={"freq": place // groups, "beam": place % groups},
-                        device_id_type=pl.DeviceIdType.MESH,
-                    )
-            if sources[block] < devices:
-                for place in range(sources[block]):
-                    pl.semaphore_signal(
-                        barrier, inc=1, device_id={"freq": place // groups, "beam": place % groups},
-                        device_id_type=pl.DeviceIdType.MESH,
-                    )
+
+    @pl.when(my_block == 0)
+    def _():
+        for step in range(1, devices):
+            signal(barrier, (my_place + devices - step) % devices)
+
+    @pl.when(my_block == 1)
+    def _():
+        for place in range(groups):
+            signal(barrier, place)
 
     lane = lax.broadcasted_iota(jnp.int32, (LANE_ROWS, LANES), 1)
     inner = lax.broadcasted_iota(jnp.int32, (LANE_ROWS, LANES), 0)
@@ -510,6 +496,8 @@
     means, scales = [], []
     for c in range(chunks):
         loads[c].wait()
+        if c == 0:
+            mask_load.wait()
         rows = slice(c * span, (c + 1) * span)
         dotted = beams // 2
         flat = jnp.concatenate([x_ref[b, rows] for b in range(dotted)], axis=1)
@@ -544,117 +532,202 @@
     fine = (channel_scale - coarse).astype(jnp.bfloat16).astype(jnp.float32)
     offset = channel_mean * (coarse + fine)
 
-    def message(block, slot, first, last):
-        beam = (my_group + slot) % beams
+    def summing(depth):
+        chosen = band_mask(depth, width)
+        matrix = jnp.concatenate(
+            [jnp.where(chosen, coarse, 0.0), jnp.where(chosen, fine, 0.0)], axis=0
+        ).astype(jnp.bfloat16)
+        shift = jnp.sum(jnp.where(chosen, offset, 0.0), axis=1, keepdims=True)
+
+        def tiles(beam):
+            both = jnp.dot(matrix, x_ref[beam], preferred_element_type=jnp.float32)
+            sums = both[:chosen.shape[0]] + both[chosen.shape[0]:] - shift
+            return [
+                [sums[t:t + LANE_ROWS, p * LANES:(p + 1) * LANES] for p in range(2)]
+                for t in range(0, chosen.shape[0], LANE_ROWS)
+            ]
+
+        return tiles
+
+    def message(block, slot, begin, end):
         return pltpu.make_async_remote_copy(
-            src_ref=send.at[block, slot, pl.ds(first, last - first)],
-            dst_ref=out_ref.at[0, my_place, pl.ds(first, last - first)],
+            src_ref=send.at[block, slot, pl.ds(begin, end - begin)],
+            dst_ref=recv.at[my_place, pl.ds(begin, end - begin)],
             send_sem=send_sem.at[block, slot],
             recv_sem=recv_sem.at[my_place],
-            device_id={"freq": block, "beam": beam},
+            device_id={"freq": block, "beam": (my_group + slot) % beams},
             device_id_type=pl.DeviceIdType.MESH,
         )
 
-    def own_copy():
-        return pltpu.make_async_copy(send.at[0, 0], out_ref.at[0, my_place], own_sem.at[0])
-
-    def outgoing(action, kind, slot):
-        if kind < 2 and slot == 0:
-            pass
-        else:
-            action(message(0, slot, *kind_span(kind)))
-        if kind == 0:
-            action(message(1, slot, 0, 8))
+    def near_messages(action, slot, narrow):
+        if narrow:
+            action(message(0, slot, *block_span(2)))
+            return
+
+        @pl.when(my_block == 1)
+        def _():
+            action(message(0, slot, *block_span(1)))
+        if slot > 0:
+            @pl.when(my_block == 0)
+            def _():
+                action(message(0, slot, *block_span(0)))
+
+    def near_phase(narrow):
+        tiles = summing(0 if narrow else 1)
+        for slot in range(beams):
+            for number, leaf in enumerate(near_leaves(tiles((my_group + slot) % beams))):
+                if leaf is not None:
+                    send[0, slot, number] = leaf.astype(jnp.bfloat16)
+                    if slot == 0 and not narrow:
+                        @pl.when(my_block == 0)
+                        def _(leaf=leaf, number=number):
+                            recv[my_place, number] = leaf.astype(jnp.bfloat16)
+            if slot == 0:
+                if narrow:
+                    pl.semaphore_wait(barrier, groups)
+                    for place in range(quarter):
+                        signal(ready_sem, place)
+                else:
+                    pl.semaphore_wait(barrier, jnp.where(my_block == 0, 2 * groups - 1, groups))
+            near_messages(lambda copy: copy.start(), slot, narrow)
+
+    def far_messages(action, slot, low):
+        action(message(1, slot, 0 if low else 4, 8))
+        if low:
             for half in range(2):
-                @pl.when((my_group * 4 >= groups) if half else (my_group * 4 < groups))
+                @pl.when((my_group * 2 >= quarter) if half else (my_group * 2 < quarter))
                 def _(half=half):
                     for block in (2, 3):
                         action(message(block, slot, 4 * half, 8))
-        if kind == 1:
-            action(message(1, slot, 4, 8))
-
-    targets = (devices - 1, 2 * groups - 1, groups, groups)
-    for kind in range(4):
-        @pl.when(kind_here == kind)
-        def _(kind=kind):
-            chosen = band_mask(kind, width)
-            rows = chosen.shape[0]
-            matrix = jnp.concatenate(
-                [jnp.where(chosen, coarse, 0.0), jnp.where(chosen, fine, 0.0)], axis=0
-            ).astype(jnp.bfloat16)
-            shift = jnp.sum(jnp.where(chosen, offset, 0.0), axis=1, keepdims=True)
-            for slot in range(beams):
-                beam = (my_group + slot) % beams
-                both = jnp.dot(matrix, x_ref[beam], preferred_element_type=jnp.float32)
-                sums = both[:rows] + both[rows:] - shift
-                tiles = [
-                    [sums[t * LANE_ROWS:(t + 1) * LANE_ROWS, p * LANES:(p + 1) * LANES] for p in range(2)]
-                    for t in range(rows // LANE_ROWS)
-                ]
-                for block, leaves in leaf_rows(kind, tiles).items():
-                    for number, leaf in enumerate(leaves):
-                        if leaf is not None:
-                            send[block, slot, number] = leaf.astype(jnp.bfloat16)
-                if slot == 0:
-                    pl.semaphore_wait(barrier, targets[kind])
-                outgoing(lambda copy: copy.start(), kind, slot)
-                if kind < 2 and slot == 0:
-                    own_copy().start()
-
-    def arrival(place, first, last):
-        target = out_ref.at[0, place, pl.ds(first, last - first)]
+
+    def far_phase(low):
+        tiles = summing(3 if low else 2)
+        if low:
+            pl.semaphore_wait(ready_sem, 2 * groups)
+        for slot in range(beams):
+            for block, leaves in far_leaves(tiles((my_group + slot) % beams)).items():
+                for number, leaf in enumerate(leaves):
+                    send[block, slot, number] = leaf.astype(jnp.bfloat16)
+            far_messages(lambda copy: copy.start(), slot, low)
+
+    def arrival(place, begin, end):
+        target = recv.at[place, pl.ds(begin, end - begin)]
         pltpu.make_async_remote_copy(
             src_ref=target, dst_ref=target, send_sem=send_sem.at[0, 0], recv_sem=recv_sem.at[place],
             device_id={"freq": my_block, "beam": my_group}, device_id_type=pl.DeviceIdType.MESH,
         ).wait_recv()
 
+    args = (recv, first, work, mid, series)
+    pitch = first.shape[1] // LANE_ROWS
+
+    def wide_places(count, numbers_of):
+        per = count // LANE_ROWS
+        return [
+            ((place // per) * pitch + (place % per) * (pitch - LANE_ROWS) // per + address, place, numbers)
+            for place in range(count) for address, numbers in numbers_of(place)
+        ]
+
+    @pl.when(my_block < 2)
+    def _():
+        near_phase(False)
+
+    @pl.when(my_block >= 2)
+    def _():
+        near_phase(True)
+
+    for low in (True, False):
+        @pl.when((my_block == 0) & ((my_group < quarter) == low))
+        def _(low=low):
+            far_phase(low)
+
+    widths_load.wait()
+
     @pl.when(my_block == 0)
     def _():
-        own_copy().wait()
-        for place in range(devices):
-            kind = max(place // groups, 0)
-            extent = kind_span(0 if kind == 0 else min(kind + 1, 3))
-
-            @pl.when(place != my_place)
-            def _(place=place, extent=extent):
-                arrival(place, *extent)
+        for place in range(groups):
+            @pl.when(place != my_group)
+            def _(place=place):
+                arrival(place, *block_span(0))
+        for place in range(groups, 2 * groups):
+            arrival(place, *block_span(1))
+        unit_rows(*args, 512, 1, 256, 1, wide_places(
+            2 * groups,
+            lambda place: [(8 * a, (a if place < groups else None, 6 + a)) for a in range(2)],
+        ))
+        for place in range(2 * groups, 4 * groups):
+            arrival(place, *block_span(2))
+        unit_rows(*args, 256, 1, 256, 0, wide_places(
+            4 * groups, lambda place: [(0, (2 if place < 2 * groups else None, 3))],
+        ))
+        unit_rows(*args, 0, 0, 256, 0, wide_places(4 * groups, lambda place: [(0, (4, 5))]))
+        result = boxcar_rows(widths_ref, series, prefix, 6)
+        unpermuted(result[:4], out_ref, 0, 0)
+        unpermuted(result[4:], out_ref, 512, 1)
 
     @pl.when(my_block == 1)
     def _():
         for place in range(groups):
-            arrival(place, *late_span(place, groups // 2))
-
-    @pl.when(my_block > 1)
-    def _():
-        for place in range(groups // 2):
-            arrival(place, *late_span(place, groups // 4))
-
-    for kind in range(4):
-        @pl.when(kind_here == kind)
-        def _(kind=kind):
-            for slot in range(beams):
-                outgoing(lambda copy: copy.wait_send(), kind, slot)
-
-
-def spread_rows(intensity, channel_mask):
+            arrival(place, *late_span(place, quarter))
+        unit_rows(*args, 0, 1, 256, 2, wide_places(
+            groups,
+            lambda place: [
+                (8 * (2 * (q % 2) + q // 2), (q if place < quarter else None, 4 + q)) for q in range(4)
+            ],
+        ))
+        unpermuted(boxcar_rows(widths_ref, series, prefix, 2), out_ref, 0, 2)
+
+    for late in (2, 3):
+        @pl.when(my_block == late)
+        def _(late=late):
+            found = []
+            for place in range(quarter):
+                arrival(place, *late_span(place, quarter // 2))
+                for q in range(4):
+                    found.append((
+                        (2 * (q % 2) + q // 2) * pitch + place * LANE_ROWS, place,
+                        (q if 2 * place < quarter else None, 4 + q),
+                    ))
+            unit_rows(*args, 0, late, 128, 2, found)
+            unpermuted(boxcar_rows(widths_ref, series, prefix, 1), out_ref, 0, 3)
+
+    for slot in range(beams):
+        for narrow in (True, False):
+            @pl.when((my_block >= 2) == narrow)
+            def _(narrow=narrow, slot=slot):
+                near_messages(lambda copy: copy.wait_send(), slot, narrow)
+        for low in (True, False):
+            @pl.when((my_block == 0) & ((my_group < quarter) == low))
+            def _(low=low, slot=slot):
+                far_messages(lambda copy: copy.wait_send(), slot, low)
+
+
+def search(intensity, channel_mask, box_widths):
     beams, width, samples = intensity.shape
     blocks, groups = lax.axis_size("freq"), lax.axis_size("beam")
     devices = blocks * groups
     return pl.pallas_call(
-        spread_kernel,
-        in_specs=[pl.BlockSpec(memory_space=pl.ANY), pl.BlockSpec(memory_space=pltpu.VMEM)],
-        out_specs=pl.BlockSpec(memory_space=pl.ANY),
+        search_kernel,
+        in_specs=[pl.BlockSpec(memory_space=pl.ANY)] * 3,
+        out_specs=pl.BlockSpec(memory_space=pltpu.VMEM),
         scratch_shapes=[
             pltpu.VMEM((beams, width, samples), jnp.bfloat16),
-            pltpu.SemaphoreType.DMA((2,)),
+            pltpu.VMEM((1, width * groups), jnp.int32),
+            pltpu.SMEM(box_widths.shape, jnp.int32),
+            pltpu.SemaphoreType.DMA((4,)),
             pltpu.VMEM((blocks, beams, 8, LANE_ROWS, LANES), jnp.bfloat16),
             pltpu.SemaphoreType.DMA((blocks, beams)),
+            pltpu.VMEM((devices, 8, LANE_ROWS, LANES), jnp.bfloat16),
             pltpu.SemaphoreType.DMA((devices,)),
-            pltpu.SemaphoreType.DMA((1,)),
+            pltpu.SemaphoreType.REGULAR,
+            pltpu.VMEM((2, samples + LANE_ROWS * LANE_ROWS, LANES), jnp.float32),
+            pltpu.VMEM((2, samples, LANES), jnp.float32),
+            pltpu.VMEM((2, samples, LANES), jnp.float32),
+            pltpu.VMEM((3 * samples, 2 * samples), jnp.bfloat16),
+            pltpu.VMEM((6, LANE_ROWS + samples + WIDEST, LANES), jnp.float32),
         ],
-        out_shape=jax.ShapeDtypeStruct((1, devices, 8, LANE_ROWS, LANES), jnp.bfloat16),
+        out_shape=jax.ShapeDtypeStruct((1, NDM // blocks), jnp.float32),
         compiler_params=pltpu.CompilerParams(collective_id=0, has_side_effects=True),
-    )(intensity, channel_mask.reshape(1, -1))
+    )(intensity, channel_mask.reshape(1, -1), box_widths)
 
 
 def ramped(pair, start, stride, far, only_late=False):
@@ -676,13 +749,13 @@
     return [a if b is None else (None if a is None else a + b) for a, b in zip(low, high)]
 
 
-def unit_rows(x_ref, first, work, mid, series, base, root, leaves, kinds, found):
+def unit_rows(recv, first, work, mid, series, base, root, leaves, kinds, found):
     tiles = leaves // LANE_ROWS
     pitch = first.shape[1] // LANE_ROWS
     for address, place, numbers in found:
         for part in range(2):
             if numbers[part] is not None:
-                first[part, address:address + LANE_ROWS] = x_ref[0, place, numbers[part]].astype(jnp.float32)
+                first[part, address:address + LANE_ROWS] = recv[place, numbers[part]].astype(jnp.float32)
 
     def leaf(tile, part):
         outer, kind = tile >> kinds, tile & ((1 << kinds) - 1)
@@ -809,89 +882,14 @@
         column = columns[number >> repeat_bits]
         spread = jnp.take_along_axis(column, picks, axis=1, mode="promise_in_bounds")
         at = offset + number * LANES
-        out_ref[0, :, at:at + LANES] = spread[:1]
-
-
-def peaks_kernel(widths_ref, x_ref, out_ref, first, work, mid, series, prefix):
-    block = lax.axis_index("freq")
-    groups = lax.axis_size("beam")
-    pitch = first.shape[1] // LANE_ROWS
-    args = (x_ref, first, work, mid, series)
-
-    def wide_places(devices, numbers_of):
-        found = []
-        per = devices // LANE_ROWS
-        for place in range(devices):
-            s, b = divmod(place, per)
-            for address, numbers in numbers_of(place):
-                found.append((s * pitch + b * (pitch - LANE_ROWS) // per + address, place, numbers))
-        return found
-
-    @pl.when(block == 0)
-    def _():
-        unit_rows(*args, 512, 1, 256, 1, wide_places(
-            2 * groups,
-            lambda place: [(8 * a, (a if place < groups else None, 6 + a)) for a in range(2)],
-        ))
-        unit_rows(*args, 256, 1, 256, 0, wide_places(
-            4 * groups, lambda place: [(0, (2 if place < 2 * groups else None, 3))],
-        ))
-        unit_rows(*args, 0, 0, 256, 0, wide_places(4 * groups, lambda place: [(0, (4, 5))]))
-        result = boxcar_rows(widths_ref, series, prefix, 6)
-        unpermuted(result[:4], out_ref, 0, 0)
-        unpermuted(result[4:], out_ref, 512, 1)
-
-    @pl.when(block == 1)
-    def _():
-        unit_rows(*args, 0, 1, 256, 2, wide_places(
-            groups,
-            lambda place: [
-                (8 * (2 * (q % 2) + q // 2), (q if 2 * place < groups else None, 4 + q)) for q in range(4)
-            ],
-        ))
-        unpermuted(boxcar_rows(widths_ref, series, prefix, 2), out_ref, 0, 2)
-
-    for late in (2, 3):
-        @pl.when(block == late)
-        def _(late=late):
-            found = []
-            for place in range(groups // 2):
-                for q in range(4):
-                    found.append((
-                        (2 * (q % 2) + q // 2) * pitch + place * LANE_ROWS, place,
-                        (q if 4 * place < groups else None, 4 + q),
-                    ))
-            unit_rows(*args, 0, late, 128, 2, found)
-            unpermuted(boxcar_rows(widths_ref, series, prefix, 1), out_ref, 0, 3)
-
-
-def beam_peaks(rows, box_widths):
-    samples = 2 * LANES
-    total = 4 * samples
-    return pl.pallas_call(
-        peaks_kernel,
-        grid_spec=pltpu.PrefetchScalarGridSpec(
-            num_scalar_prefetch=1,
-            grid=(1,),
-            in_specs=[pl.BlockSpec(rows.shape, lambda b, w: (0, 0, 0, 0, 0))],
-            out_specs=pl.BlockSpec((1, 1, total), lambda b, w: (0, 0, 0)),
-            scratch_shapes=[
-                pltpu.VMEM((2, samples + LANE_ROWS * LANE_ROWS, LANES), jnp.float32),
-                pltpu.VMEM((2, samples, LANES), jnp.float32),
-                pltpu.VMEM((2, samples, LANES), jnp.float32),
-                pltpu.VMEM((3 * samples, 2 * samples), jnp.bfloat16),
-                pltpu.VMEM((6, LANE_ROWS + samples + WIDEST, LANES), jnp.float32),
-            ],
-        ),
-        out_shape=jax.ShapeDtypeStruct((1, 1, total), jnp.float32),
-    )(box_widths, rows)[:, 0]
+        out_ref[:, at:at + LANES] = spread[:1]
 
 
 def shards(intensity, channel_mask, box_widths):
     beams, width, samples = intensity.shape
     blocks, groups = lax.axis_size("freq"), lax.axis_size("beam")
     if compact(samples, blocks * groups, blocks, groups, beams, width):
-        return beam_peaks(spread_rows(intensity, channel_mask), box_widths)
+        return search(intensity, channel_mask, box_widths)
     rows = entry_rows(intensity, channel_mask)
     return trial_peaks(rows, box_widths, lax.axis_index("freq").reshape(1))
 

time: 25.4 us -> 22.8 us (0.90)
  the two profiles are of different devices: /device:TPU:0 before, /device:TPU:15 now
where the time goes in v2:
time: 22.8 us; the launch traced here: 22.7 us
  Pallas kernels  21.4 us (94%)
  local copies, waits for them, and re-layouts  1.28 us (6%)
    pallas_call x1, Pallas kernels, search(): pl.pallas_call(search_kernel, in_specs=[pl.BlockSpec(memory_space=pl.ANY)...  21.4 us
    unnamed x1, local copies, waits for them, and re-layouts  1.28 us

profile of v2, /device:TPU:15, one launch (start us, length us, event | category | flops | bytes accessed | tf_op | source)
XLA Modules:
  0.0 22.7 jit_solution(7144295030908674680)
XLA Ops:
  0.0 21.4 %shard_map.37 = f32[1,1024]{1,0:T(1,128)} custom-call(bf16[8,512,256]{2,1,0:T(8,128)(2,1)} %x_hbm.1, s32[1,4096]{1,0:T(1,128)} %bitcast.1, s32[9]{0:T(128)} %widths_hbm.1), custom_call_target="tpu_custom_call" | custom-call | tf_op jit(solution)/shard_map/pallas_call | solution.py:708
  21.4 1.3 %copy.5 = f32[1,1024]{1,0:T(1,128)} copy(f32[1,1024]{1,0:T(1,128)} %shard_map.37) | data formatting | bytes 8192

commit v3 on v2

--- a/solution.py
+++ b/solution.py
@@ -406,10 +406,11 @@
 def stepped(pair, amount):
     if amount == 0:
         return list(pair)
-    lane = lane_index(pair[0].shape)
+    lane = lane_index(pair[1].shape)
     near = lane < LANES - amount
-    turned = [pltpu.roll(piece, LANES - amount, 1) for piece in pair]
-    return [jnp.where(near, turned[0], turned[1]), jnp.where(near, turned[1], 0.0)]
+    turned = [None if piece is None else pltpu.roll(piece, LANES - amount, 1) for piece in pair]
+    early = None if turned[0] is None else jnp.where(near, turned[0], turned[1])
+    return [early, jnp.where(near, turned[1], 0.0)]
 
 
 def plus(low, high):
@@ -444,7 +445,7 @@
 
 def search_kernel(
     x_hbm, mask_hbm, widths_hbm, out_ref, x_ref, mask_ref, widths_ref, in_sem, send, send_sem, recv, recv_sem,
-    ready_sem, first, work, mid, series, prefix,
+    ready_sem, first, work, mid, planes, lower, series, prefix,
 ):
     beams, width, samples = x_ref.shape
     blocks, groups = lax.axis_size("freq"), lax.axis_size("beam")
@@ -488,6 +489,16 @@
     def _():
         for place in range(groups):
             signal(barrier, place)
+
+    @pl.when(my_block >= 2)
+    def _():
+        pl.semaphore_wait(barrier, groups)
+        for place in range(quarter):
+            signal(ready_sem, place)
+
+    for column in range(prefix.shape[0]):
+        prefix[column, :LANE_ROWS] = jnp.zeros((LANE_ROWS, LANES), jnp.float32)
+        prefix[column, LANE_ROWS + samples:] = jnp.full((WIDEST, LANES), -jnp.inf, jnp.float32)
 
     lane = lax.broadcasted_iota(jnp.int32, (LANE_ROWS, LANES), 1)
     inner = lax.broadcasted_iota(jnp.int32, (LANE_ROWS, LANES), 0)
@@ -535,13 +546,15 @@
     def summing(depth):
         chosen = band_mask(depth, width)
         matrix = jnp.concatenate(
-            [jnp.where(chosen, coarse, 0.0), jnp.where(chosen, fine, 0.0)], axis=0
+            [jnp.where(chosen, coarse, 0.0), jnp.where(chosen, fine, 0.0)], axis=1
         ).astype(jnp.bfloat16)
         shift = jnp.sum(jnp.where(chosen, offset, 0.0), axis=1, keepdims=True)
 
-        def tiles(beam):
-            both = jnp.dot(matrix, x_ref[beam], preferred_element_type=jnp.float32)
-            sums = both[:chosen.shape[0]] + both[chosen.shape[0]:] - shift
+        def tiles(slot):
+            rows = x_ref[(my_group + slot) % beams]
+            sums = jnp.dot(
+                matrix, jnp.concatenate([rows, rows], axis=0), preferred_element_type=jnp.float32
+            ) - shift
             return [
                 [sums[t:t + LANE_ROWS, p * LANES:(p + 1) * LANES] for p in range(2)]
                 for t in range(0, chosen.shape[0], LANE_ROWS)
@@ -574,22 +587,21 @@
 
     def near_phase(narrow):
         tiles = summing(0 if narrow else 1)
-        for slot in range(beams):
-            for number, leaf in enumerate(near_leaves(tiles((my_group + slot) % beams))):
-                if leaf is not None:
-                    send[0, slot, number] = leaf.astype(jnp.bfloat16)
-                    if slot == 0 and not narrow:
-                        @pl.when(my_block == 0)
-                        def _(leaf=leaf, number=number):
-                            recv[my_place, number] = leaf.astype(jnp.bfloat16)
-            if slot == 0:
-                if narrow:
-                    pl.semaphore_wait(barrier, groups)
-                    for place in range(quarter):
-                        signal(ready_sem, place)
-                else:
-                    pl.semaphore_wait(barrier, jnp.where(my_block == 0, 2 * groups - 1, groups))
-            near_messages(lambda copy: copy.start(), slot, narrow)
+        batch = 4
+        for begin in range(0, beams, batch):
+            slots = range(begin, begin + batch)
+            for slot, summed in [(slot, tiles(slot)) for slot in slots]:
+                for number, leaf in enumerate(near_leaves(summed)):
+                    if leaf is not None:
+                        send[0, slot, number] = leaf.astype(jnp.bfloat16)
+                if slot == 0 and not narrow:
+                    @pl.when(my_block == 0)
+                    def _():
+                        recv[my_place] = send[0, 0]
+            if begin == 0 and not narrow:
+                pl.semaphore_wait(barrier, jnp.where(my_block == 0, 2 * groups - 1, groups))
+            for slot in slots:
+                near_messages(lambda copy: copy.start(), slot, narrow)
 
     def far_messages(action, slot, low):
         action(message(1, slot, 0 if low else 4, 8))
@@ -602,13 +614,20 @@
 
     def far_phase(low):
         tiles = summing(3 if low else 2)
-        if low:
-            pl.semaphore_wait(ready_sem, 2 * groups)
-        for slot in range(beams):
-            for block, leaves in far_leaves(tiles((my_group + slot) % beams)).items():
-                for number, leaf in enumerate(leaves):
-                    send[block, slot, number] = leaf.astype(jnp.bfloat16)
-            far_messages(lambda copy: copy.start(), slot, low)
+        batch = 2
+        for begin in range(0, beams, batch):
+            slots = range(begin, begin + batch)
+            for slot, summed in [(slot, tiles(slot)) for slot in slots]:
+                for block, leaves in far_leaves(summed).items():
+                    for number, leaf in enumerate(leaves):
+                        send[block, slot, number] = leaf.astype(jnp.bfloat16)
+            if low and begin < 2:
+                continue
+            if low and begin == 2:
+                pl.semaphore_wait(ready_sem, 2 * groups)
+                slots = range(begin + batch)
+            for slot in slots:
+                far_messages(lambda copy: copy.start(), slot, low)
 
     def arrival(place, begin, end):
         target = recv.at[place, pl.ds(begin, end - begin)]
@@ -650,19 +669,28 @@
                 arrival(place, *block_span(0))
         for place in range(groups, 2 * groups):
             arrival(place, *block_span(1))
-        unit_rows(*args, 512, 1, 256, 1, wide_places(
+        unit_rows(*args, 0, 1, 256, 1, wide_places(
             2 * groups,
             lambda place: [(8 * a, (a if place < groups else None, 6 + a)) for a in range(2)],
         ))
-        for place in range(2 * groups, 4 * groups):
-            arrival(place, *block_span(2))
-        unit_rows(*args, 256, 1, 256, 0, wide_places(
-            4 * groups, lambda place: [(0, (2 if place < 2 * groups else None, 3))],
-        ))
-        unit_rows(*args, 0, 0, 256, 0, wide_places(4 * groups, lambda place: [(0, (4, 5))]))
-        result = boxcar_rows(widths_ref, series, prefix, 6)
-        unpermuted(result[:4], out_ref, 0, 0)
-        unpermuted(result[4:], out_ref, 512, 1)
+        for plane in range(2):
+            for root in range(2):
+                numbers = (4 - 2 * root, 5 - 2 * root)
+                plane_rows(recv, first, mid, planes.at[root], plane, groups, root, numbers)
+        for root in range(2):
+            lower_rows(planes.at[root], lower.at[root], root)
+        unpermuted(boxcar_rows(widths_ref, series, prefix, 0, 2), out_ref, 512, 1)
+        for plane in range(2, blocks):
+            for place in range(plane * groups, (plane + 1) * groups):
+                arrival(place, *block_span(2))
+            for root in range(2):
+                numbers = (4, 5) if root == 0 else (None, 3)
+                plane_rows(recv, first, mid, planes.at[root], plane, groups, root, numbers)
+        for root in range(2):
+            upper_rows(planes.at[root], lower.at[root], series, 256 * (1 + root), root)
+        result = boxcar_rows(widths_ref, series, prefix, 2, 4)
+        unfolded(result[:2], out_ref, 0)
+        unfolded(result[2:], out_ref, 256)
 
     @pl.when(my_block == 1)
     def _():
@@ -674,7 +702,7 @@
                 (8 * (2 * (q % 2) + q // 2), (q if place < quarter else None, 4 + q)) for q in range(4)
             ],
         ))
-        unpermuted(boxcar_rows(widths_ref, series, prefix, 2), out_ref, 0, 2)
+        unpermuted(boxcar_rows(widths_ref, series, prefix, 0, 2), out_ref, 0, 2)
 
     for late in (2, 3):
         @pl.when(my_block == late)
@@ -688,7 +716,7 @@
                         (q if 2 * place < quarter else None, 4 + q),
                     ))
             unit_rows(*args, 0, late, 128, 2, found)
-            unpermuted(boxcar_rows(widths_ref, series, prefix, 1), out_ref, 0, 3)
+            unpermuted(boxcar_rows(widths_ref, series, prefix, 0, 1), out_ref, 0, 3)
 
     for slot in range(beams):
         for narrow in (True, False):
@@ -713,7 +741,7 @@
             pltpu.VMEM((beams, width, samples), jnp.bfloat16),
             pltpu.VMEM((1, width * groups), jnp.int32),
             pltpu.SMEM(box_widths.shape, jnp.int32),
-            pltpu.SemaphoreType.DMA((4,)),
+            pltpu.SemaphoreType.DMA((6,)),
             pltpu.VMEM((blocks, beams, 8, LANE_ROWS, LANES), jnp.bfloat16),
             pltpu.SemaphoreType.DMA((blocks, beams)),
             pltpu.VMEM((devices, 8, LANE_ROWS, LANES), jnp.bfloat16),
@@ -722,6 +750,8 @@
             pltpu.VMEM((2, samples + LANE_ROWS * LANE_ROWS, LANES), jnp.float32),
             pltpu.VMEM((2, samples, LANES), jnp.float32),
             pltpu.VMEM((2, samples, LANES), jnp.float32),
+            pltpu.VMEM((2, blocks, 2, LANE_ROWS * LANE_ROWS, LANES), jnp.float32),
+            pltpu.VMEM((2, 2, LANES, LANES), jnp.float32),
             pltpu.VMEM((3 * samples, 2 * samples), jnp.bfloat16),
             pltpu.VMEM((6, LANE_ROWS + samples + WIDEST, LANES), jnp.float32),
         ],
@@ -812,64 +842,140 @@
                 for part in range(2)
             ]
             tree.append([pair])
-        start, stride = root * tiles + g * LANE_ROWS, 1
-        while len(tree) > 1:
-            last = len(tree) == 2
-            merged = []
-            for number in range(len(tree) // 2):
-                low, high = tree[2 * number], tree[2 * number + 1]
-                rows = []
-                for r in range(2 * len(low)):
-                    source = r // 2
-                    begin = start + source + r % 2
-                    missing = high[source][0] is None
-                    moved = ramped(high[source], begin, stride, far and last, missing)
-                    rows.append(joined_pair(low[source], moved))
-                merged.append(rows)
-            tree = merged
-            start, stride = start * 2, stride * 2
+        rows = merged_rows(tree, root * tiles + g * LANE_ROWS, 1, far)
         for k in range(0, LANE_ROWS, 2):
-            rows = jnp.concatenate(
-                [jnp.concatenate(tree[0][k + half], axis=1) for half in range(2)], axis=0
-            )
-            coarse = rows.astype(jnp.bfloat16)
-            at = base + g * 64 + k * LANE_ROWS
-            samples = rows.shape[1]
-            series[at:at + 2 * LANE_ROWS, :samples] = coarse
-            series[at:at + 2 * LANE_ROWS, samples:] = (rows - coarse.astype(jnp.float32)).astype(jnp.bfloat16)
-
-
-def boxcar_rows(widths_ref, series, prefix, columns):
+            save_series(series, base + g * LANE_ROWS * LANE_ROWS + k * LANE_ROWS, rows[k:k + 2])
+
+
+def merged_rows(tree, start, stride, far):
+    while len(tree) > 1:
+        tree = [
+            [
+                joined_pair(
+                    low[r // 2],
+                    ramped(
+                        high[r // 2], start + r // 2 + r % 2, stride, far and len(tree) == 2,
+                        high[r // 2][0] is None,
+                    ),
+                )
+                for r in range(2 * len(low))
+            ]
+            for low, high in zip(tree[0::2], tree[1::2])
+        ]
+        start, stride = start * 2, stride * 2
+    return tree[0]
+
+
+def plane_rows(recv, first, mid, target, plane, groups, root, numbers):
+    parts = [part for part in range(2) if numbers[part] is not None]
+    for place in range(groups):
+        for part in parts:
+            at = place * LANE_ROWS
+            first[part, at:at + LANE_ROWS] = recv[plane * groups + place, numbers[part]].astype(jnp.float32)
+    tree = [
+        [[first[part, pl.ds(j, LANE_ROWS, stride=LANE_ROWS)] if part in parts else None for part in range(2)]]
+        for j in range(LANE_ROWS)
+    ]
+    level_root = root
+    while len(tree) > 1:
+        tree = [
+            [
+                joined_pair(low[r // 2], stepped(high[r // 2], level_root + r // 2 + r % 2))
+                for r in range(2 * len(low))
+            ]
+            for low, high in zip(tree[0::2], tree[1::2])
+        ]
+        level_root = level_root * 2
+    for j, pair in enumerate(tree[0]):
+        for part in parts:
+            mid[part, j * LANE_ROWS:(j + 1) * LANE_ROWS] = pair[part]
+    tree = [
+        [[mid[part, pl.ds(p, LANE_ROWS, stride=LANE_ROWS)] if part in parts else None for part in range(2)]]
+        for p in range(LANE_ROWS)
+    ]
+    for k, pair in enumerate(merged_rows(tree, root * LANE_ROWS, 1, False)):
+        for part in parts:
+            target[plane, part, k * LANE_ROWS:(k + 1) * LANE_ROWS] = pair[part]
+
+
+def plane_tile(target, plane, k, parts):
+    return [
+        target[plane, part, k * LANE_ROWS:(k + 1) * LANE_ROWS] if part in parts else None for part in range(2)
+    ]
+
+
+def lower_rows(target, lower, root):
+    for k in range(LANE_ROWS):
+        tree = [[plane_tile(target, plane, k, (0, 1))] for plane in range(2)]
+        for q, pair in enumerate(merged_rows(tree, root * LANE_ROWS * LANE_ROWS + k, LANE_ROWS, False)):
+            for part in range(2):
+                at = (2 * k + q) * LANE_ROWS
+                lower[part, at:at + LANE_ROWS] = pair[part]
+
+
+def upper_rows(target, lower, series, base, root):
+    parts = (0, 1) if root == 0 else (1,)
+    for k in range(LANE_ROWS):
+        begin = root * LANE_ROWS * LANE_ROWS + k
+        high = merged_rows([[plane_tile(target, plane, k, parts)] for plane in (2, 3)], begin, LANE_ROWS, False)
+        low = []
+        for q in range(2):
+            at = (2 * k + q) * LANE_ROWS
+            low.append([lower[part, at:at + LANE_ROWS] for part in range(2)])
+        rows = merged_rows([low, high], begin * 2, 2 * LANE_ROWS, root > 0)
+        for number in range(0, 4, 2):
+            save_series(series, base + (4 * k + number) * LANE_ROWS, rows[number:number + 2])
+
+
+def save_series(series, at, pairs):
+    rows = jnp.concatenate([jnp.concatenate(pair, axis=1) for pair in pairs], axis=0)
+    coarse = rows.astype(jnp.bfloat16)
+    samples = rows.shape[1]
+    series[at:at + 2 * LANE_ROWS, :samples] = coarse
+    series[at:at + 2 * LANE_ROWS, samples:] = (rows - coarse.astype(jnp.float32)).astype(jnp.bfloat16)
+
+
+def unfolded(columns, out_ref, offset):
+    lane = lane_index((LANE_ROWS, LANES))
+    for number in range(2):
+        picks = (lane & 15) * LANE_ROWS + (lane >> 5) + 4 * number
+        spread = [jnp.take_along_axis(column, picks, axis=1, mode="promise_in_bounds") for column in columns]
+        at = offset + number * LANES
+        out_ref[:, at:at + LANES] = jnp.where(lane & 16 == 0, spread[0], spread[1])[:1]
+
+
+def boxcar_rows(widths_ref, series, prefix, begin, count):
     lanes = prefix.shape[2]
     samples = series.shape[1] // 2
     until = lax.broadcasted_iota(jnp.int32, (samples, 2 * samples), 0)
     time = lax.broadcasted_iota(jnp.int32, (samples, 2 * samples), 1) & (samples - 1)
     ladder = jnp.where(time <= until, 1.0, 0.0).astype(jnp.bfloat16)
-    margin = prefix.shape[1] - samples - LANE_ROWS
-    piece = min(2, columns)
-    for part in range(columns // piece):
+    piece = min(2, count)
+    for start in range(begin, begin + count, piece):
         sums = lax.dot_general(
-            ladder, series[part * piece * lanes:(part + 1) * piece * lanes], (((1,), (1,)), ((), ())),
+            ladder, series[start * lanes:(start + piece) * lanes], (((1,), (1,)), ((), ())),
             preferred_element_type=jnp.float32,
         )
         for side in range(piece):
-            column = piece * part + side
-            prefix[column, :LANE_ROWS] = jnp.zeros((LANE_ROWS, lanes), jnp.float32)
-            prefix[column, LANE_ROWS:LANE_ROWS + samples] = sums[:, side * lanes:(side + 1) * lanes]
-            prefix[column, LANE_ROWS + samples:] = jnp.full((margin, lanes), -jnp.inf, jnp.float32)
+            prefix[start + side, LANE_ROWS:LANE_ROWS + samples] = sums[:, side * lanes:(side + 1) * lanes]
+    widths = [widths_ref[number] for number in range(widths_ref.shape[0])]
+    norms = [
+        lax.rsqrt(jnp.full((LANE_ROWS, lanes), width * CHANS, jnp.int32).astype(jnp.float32)) for width in widths
+    ]
     result = []
-    for column in range(columns):
-        best = None
-        for number in range(widths_ref.shape[0]):
-            width = widths_ref[number]
-            sums = (
-                prefix[column, pl.ds(LANE_ROWS - 1 + width, samples)]
-                - prefix[column, LANE_ROWS - 1:LANE_ROWS - 1 + samples]
-            )
-            norm = lax.rsqrt(jnp.full((1, lanes), width * CHANS, jnp.int32).astype(jnp.float32))
-            peak = jnp.max(sums, axis=0, keepdims=True) * norm
-            best = peak if best is None else jnp.maximum(best, peak)
-        result.append(jnp.broadcast_to(best, (LANE_ROWS, lanes)))
+    for column in range(begin, begin + count):
+        ahead = [prefix[column, pl.ds(LANE_ROWS - 1 + width, samples)] for width in widths]
+        base = prefix[column, LANE_ROWS - 1:LANE_ROWS - 1 + samples]
+        best = [None] * len(widths)
+        for at in range(0, samples, LANE_ROWS):
+            before = base[at:at + LANE_ROWS]
+            for number, after in enumerate(ahead):
+                gain = after[at:at + LANE_ROWS] - before
+                best[number] = gain if at == 0 else jnp.maximum(best[number], gain)
+        peak = best[0] * norms[0]
+        for value, norm in zip(best[1:], norms[1:]):
+            peak = jnp.maximum(peak, value * norm)
+        result.append(jnp.broadcast_to(jnp.max(peak, axis=0, keepdims=True), (LANE_ROWS, lanes)))
     return result
 
 

time: 22.8 us -> 21.3 us (0.934)
  the two profiles are of different devices: /device:TPU:15 before, /device:TPU:0 now
where the time goes in v3:
time: 21.3 us; the launch traced here: 21.1 us
  Pallas kernels  19.8 us (93%)
  local copies, waits for them, and re-layouts  1.28 us (6%)
    pallas_call x1, Pallas kernels, search(): pl.pallas_call(search_kernel, in_specs=[pl.BlockSpec(memory_space=pl.ANY)...  19.8 us
    unnamed x1, local copies, waits for them, and re-layouts  1.28 us

profile of v3, /device:TPU:0, one launch (start us, length us, event | category | flops | bytes accessed | tf_op | source)
XLA Modules:
  0.0 21.1 jit_solution(15148225636126116860)
XLA Ops:
  0.0 19.8 %shard_map.37 = f32[1,1024]{1,0:T(1,128)} custom-call(bf16[8,512,256]{2,1,0:T(8,128)(2,1)} %x_hbm.1, s32[1,4096]{1,0:T(1,128)} %bitcast.1, s32[9]{0:T(128)} %widths_hbm.1), custom_call_target="tpu_custom_call" | custom-call | tf_op jit(solution)/shard_map/pallas_call | solution.py:736
  19.8 1.3 %copy.5 = f32[1,1024]{1,0:T(1,128)} copy(f32[1,1024]{1,0:T(1,128)} %shard_map.37) | data formatting | bytes 8192

commit v4 on v3

--- a/solution.py
+++ b/solution.py
@@ -444,8 +444,8 @@
 
 
 def search_kernel(
-    x_hbm, mask_hbm, widths_hbm, out_ref, x_ref, mask_ref, widths_ref, in_sem, send, send_sem, recv, recv_sem,
-    ready_sem, first, work, mid, planes, lower, series, prefix,
+    x_hbm, mask_hbm, widths_hbm, out_ref, x_ref, unit_ref, mask_ref, widths_ref, in_sem, send, send_sem, recv, recv_sem,
+    ready_sem, first, work, mid, planes, double, lower, series, prefix,
 ):
     beams, width, samples = x_ref.shape
     blocks, groups = lax.axis_size("freq"), lax.axis_size("beam")
@@ -502,37 +502,30 @@
 
     lane = lax.broadcasted_iota(jnp.int32, (LANE_ROWS, LANES), 1)
     inner = lax.broadcasted_iota(jnp.int32, (LANE_ROWS, LANES), 0)
-    ones = jnp.ones((2 * LANE_ROWS, samples), jnp.bfloat16)
-    dims = (((1,), (1,)), ((), ()))
+    unit_ref[...] = jnp.ones(unit_ref.shape, jnp.bfloat16)
     means, scales = [], []
     for c in range(chunks):
         loads[c].wait()
         if c == 0:
             mask_load.wait()
-        rows = slice(c * span, (c + 1) * span)
-        dotted = beams // 2
-        flat = jnp.concatenate([x_ref[b, rows] for b in range(dotted)], axis=1)
-        rest = jnp.concatenate([x_ref[b, rows] for b in range(dotted, beams)], axis=1)
-        gram = lax.dot_general(flat, flat, dims, preferred_element_type=jnp.float32)
-        total = lax.dot_general(
-            jnp.concatenate([ones] * beams, axis=1), jnp.concatenate([flat, rest], axis=1), dims,
-            preferred_element_type=jnp.float32,
-        )[:1]
-        squares = []
+        unit = unit_ref[...].astype(jnp.float32)
+        totals = []
         for column in range(span // LANES):
-            sums = jnp.zeros((LANE_ROWS, LANES), jnp.float32)
-            for tile in range(LANES // LANE_ROWS):
-                at = column * LANES + tile * LANE_ROWS
-                own = jnp.zeros((LANE_ROWS, samples), jnp.float32)
-                for b in range(dotted, beams):
-                    wide = x_ref[b, c * span + at:c * span + at + LANE_ROWS].astype(jnp.float32)
-                    own = own + wide * wide
-                own = jnp.sum(own, axis=1, keepdims=True)
-                both = gram[at:at + LANE_ROWS, column * LANES:(column + 1) * LANES] + own
-                sums = sums + jnp.where(lane == inner + tile * LANE_ROWS, both, 0.0)
-            squares.append(jnp.sum(sums, axis=0, keepdims=True))
-        mean = total / row_total
-        var = jnp.concatenate(squares, axis=1) / row_total - mean * mean
+            found = [jnp.zeros((LANE_ROWS, LANES), jnp.float32) for _ in range(2)]
+            for pair in range(LANES // (2 * LANE_ROWS)):
+                at = c * span + column * LANES + pair * 2 * LANE_ROWS
+                sums = [jnp.zeros((2 * LANE_ROWS, samples), jnp.float32) for _ in range(2)]
+                for b in range(beams):
+                    wide = x_ref[b, at:at + 2 * LANE_ROWS].astype(jnp.float32)
+                    sums = [sums[0] + wide * unit, sums[1] + wide * wide]
+                sums = [jnp.sum(value, axis=1, keepdims=True) for value in sums]
+                for half in range(2):
+                    spot = lane == inner + (2 * pair + half) * LANE_ROWS
+                    cut = slice(half * LANE_ROWS, (half + 1) * LANE_ROWS)
+                    found = [have + jnp.where(spot, value[cut], 0.0) for have, value in zip(found, sums)]
+            totals.append([jnp.sum(value, axis=0, keepdims=True) for value in found])
+        mean = jnp.concatenate([total[0] for total in totals], axis=1) / row_total
+        var = jnp.concatenate([total[1] for total in totals], axis=1) / row_total - mean * mean
         place = pl.multiple_of(my_group * width + c * span, span)
         clean = mask_ref[:, pl.ds(place, span)].astype(jnp.float32)
         means.append(mean)
@@ -603,14 +596,15 @@
             for slot in slots:
                 near_messages(lambda copy: copy.start(), slot, narrow)
 
-    def far_messages(action, slot, low):
+    def next_messages(action, slot, low):
         action(message(1, slot, 0 if low else 4, 8))
-        if low:
-            for half in range(2):
-                @pl.when((my_group * 2 >= quarter) if half else (my_group * 2 < quarter))
-                def _(half=half):
-                    for block in (2, 3):
-                        action(message(block, slot, 4 * half, 8))
+
+    def last_messages(action, slot):
+        for half in range(2):
+            @pl.when((my_group * 2 >= quarter) if half else (my_group * 2 < quarter))
+            def _(half=half):
+                for block in (3, 2):
+                    action(message(block, slot, 4 * half, 8))
 
     def far_phase(low):
         tiles = summing(3 if low else 2)
@@ -621,13 +615,12 @@
                 for block, leaves in far_leaves(summed).items():
                     for number, leaf in enumerate(leaves):
                         send[block, slot, number] = leaf.astype(jnp.bfloat16)
-            if low and begin < 2:
-                continue
-            if low and begin == 2:
-                pl.semaphore_wait(ready_sem, 2 * groups)
-                slots = range(begin + batch)
             for slot in slots:
-                far_messages(lambda copy: copy.start(), slot, low)
+                next_messages(lambda copy: copy.start(), slot, low)
+        if low:
+            pl.semaphore_wait(ready_sem, 2 * groups)
+            for slot in range(beams):
+                last_messages(lambda copy: copy.start(), slot)
 
     def arrival(place, begin, end):
         target = recv.at[place, pl.ds(begin, end - begin)]
@@ -667,24 +660,23 @@
             @pl.when(place != my_group)
             def _(place=place):
                 arrival(place, *block_span(0))
+        plane_rows(recv, first, mid, double, 0, groups, 1, ((0, 6), (1, 7)))
+        for root in range(2):
+            plane_rows(recv, first, mid, planes.at[root], 0, groups, root, ((4 - 2 * root, 5 - 2 * root),))
         for place in range(groups, 2 * groups):
             arrival(place, *block_span(1))
-        unit_rows(*args, 0, 1, 256, 1, wide_places(
-            2 * groups,
-            lambda place: [(8 * a, (a if place < groups else None, 6 + a)) for a in range(2)],
-        ))
-        for plane in range(2):
-            for root in range(2):
-                numbers = (4 - 2 * root, 5 - 2 * root)
-                plane_rows(recv, first, mid, planes.at[root], plane, groups, root, numbers)
+        plane_rows(recv, first, mid, double, 1, groups, 1, ((None, 6), (None, 7)))
+        double_rows(double, series, 0)
+        for root in range(2):
+            plane_rows(recv, first, mid, planes.at[root], 1, groups, root, ((4 - 2 * root, 5 - 2 * root),))
         for root in range(2):
             lower_rows(planes.at[root], lower.at[root], root)
-        unpermuted(boxcar_rows(widths_ref, series, prefix, 0, 2), out_ref, 512, 1)
+        unpermuted(boxcar_rows(widths_ref, series, prefix, 0, 2), out_ref, 512, 1, 4)
         for plane in range(2, blocks):
             for place in range(plane * groups, (plane + 1) * groups):
                 arrival(place, *block_span(2))
             for root in range(2):
-                numbers = (4, 5) if root == 0 else (None, 3)
+                numbers = ((4, 5) if root == 0 else (None, 3),)
                 plane_rows(recv, first, mid, planes.at[root], plane, groups, root, numbers)
         for root in range(2):
             upper_rows(planes.at[root], lower.at[root], series, 256 * (1 + root), root)
@@ -702,7 +694,7 @@
                 (8 * (2 * (q % 2) + q // 2), (q if place < quarter else None, 4 + q)) for q in range(4)
             ],
         ))
-        unpermuted(boxcar_rows(widths_ref, series, prefix, 0, 2), out_ref, 0, 2)
+        unpermuted(boxcar_rows(widths_ref, series, prefix, 0, 2), out_ref, 0, 2, 3)
 
     for late in (2, 3):
         @pl.when(my_block == late)
@@ -716,7 +708,7 @@
                         (q if 2 * place < quarter else None, 4 + q),
                     ))
             unit_rows(*args, 0, late, 128, 2, found)
-            unpermuted(boxcar_rows(widths_ref, series, prefix, 0, 1), out_ref, 0, 3)
+            unpermuted(boxcar_rows(widths_ref, series, prefix, 0, 1), out_ref, 0, 3, 3)
 
     for slot in range(beams):
         for narrow in (True, False):
@@ -726,19 +718,23 @@
         for low in (True, False):
             @pl.when((my_block == 0) & ((my_group < quarter) == low))
             def _(low=low, slot=slot):
-                far_messages(lambda copy: copy.wait_send(), slot, low)
+                next_messages(lambda copy: copy.wait_send(), slot, low)
+                if low:
+                    last_messages(lambda copy: copy.wait_send(), slot)
 
 
 def search(intensity, channel_mask, box_widths):
     beams, width, samples = intensity.shape
     blocks, groups = lax.axis_size("freq"), lax.axis_size("beam")
     devices = blocks * groups
+    operands = (intensity, channel_mask.reshape(1, -1), box_widths)
     return pl.pallas_call(
         search_kernel,
         in_specs=[pl.BlockSpec(memory_space=pl.ANY)] * 3,
         out_specs=pl.BlockSpec(memory_space=pltpu.VMEM),
         scratch_shapes=[
             pltpu.VMEM((beams, width, samples), jnp.bfloat16),
+            pltpu.VMEM((2 * LANE_ROWS, samples), jnp.bfloat16),
             pltpu.VMEM((1, width * groups), jnp.int32),
             pltpu.SMEM(box_widths.shape, jnp.int32),
             pltpu.SemaphoreType.DMA((6,)),
@@ -752,12 +748,13 @@
             pltpu.VMEM((2, samples, LANES), jnp.float32),
             pltpu.VMEM((2, blocks, 2, LANE_ROWS * LANE_ROWS, LANES), jnp.float32),
             pltpu.VMEM((2, 2, LANES, LANES), jnp.float32),
+            pltpu.VMEM((2, 2, LANES, LANES), jnp.float32),
             pltpu.VMEM((3 * samples, 2 * samples), jnp.bfloat16),
             pltpu.VMEM((6, LANE_ROWS + samples + WIDEST, LANES), jnp.float32),
         ],
         out_shape=jax.ShapeDtypeStruct((1, NDM // blocks), jnp.float32),
-        compiler_params=pltpu.CompilerParams(collective_id=0, has_side_effects=True),
-    )(intensity, channel_mask.reshape(1, -1), box_widths)
+        compiler_params=pltpu.CompilerParams(collective_id=0, has_side_effects=True, vmem_limit_bytes=32 << 20),
+    )(*[pltpu.with_memory_space_constraint(value, pltpu.HBM) for value in operands])
 
 
 def ramped(pair, start, stride, far, only_late=False):
@@ -867,15 +864,19 @@
 
 
 def plane_rows(recv, first, mid, target, plane, groups, root, numbers):
-    parts = [part for part in range(2) if numbers[part] is not None]
+    kinds = len(numbers)
+    parts = [part for part in range(2) if numbers[0][part] is not None]
+    flat = LANE_ROWS * LANE_ROWS
     for place in range(groups):
-        for part in parts:
-            at = place * LANE_ROWS
-            first[part, at:at + LANE_ROWS] = recv[plane * groups + place, numbers[part]].astype(jnp.float32)
-    tree = [
-        [[first[part, pl.ds(j, LANE_ROWS, stride=LANE_ROWS)] if part in parts else None for part in range(2)]]
-        for j in range(LANE_ROWS)
-    ]
+        for kind in range(kinds):
+            for part in parts:
+                at = kind * flat + place * LANE_ROWS
+                first[part, at:at + LANE_ROWS] = recv[plane * groups + place, numbers[kind][part]].astype(jnp.float32)
+
+    def pair_at(source, start):
+        return [source[part, pl.ds(start, LANE_ROWS, stride=LANE_ROWS)] if part in parts else None for part in range(2)]
+
+    tree = [[pair_at(first, (tile % kinds) * flat + tile // kinds)] for tile in range(kinds * LANE_ROWS)]
     level_root = root
     while len(tree) > 1:
         tree = [
@@ -889,13 +890,21 @@
     for j, pair in enumerate(tree[0]):
         for part in parts:
             mid[part, j * LANE_ROWS:(j + 1) * LANE_ROWS] = pair[part]
-    tree = [
-        [[mid[part, pl.ds(p, LANE_ROWS, stride=LANE_ROWS)] if part in parts else None for part in range(2)]]
-        for p in range(LANE_ROWS)
-    ]
-    for k, pair in enumerate(merged_rows(tree, root * LANE_ROWS, 1, False)):
-        for part in parts:
-            target[plane, part, k * LANE_ROWS:(k + 1) * LANE_ROWS] = pair[part]
+    for g in range(kinds):
+        tree = [[pair_at(mid, g * flat + p)] for p in range(LANE_ROWS)]
+        for k, pair in enumerate(merged_rows(tree, (root * kinds + g) * LANE_ROWS, 1, False)):
+            at = g * flat + k * LANE_ROWS
+            for part in parts:
+                target[plane, part, at:at + LANE_ROWS] = pair[part]
+
+
+def double_rows(target, series, base):
+    for g in range(2):
+        for k in range(LANE_ROWS):
+            number = g * LANE_ROWS + k
+            tree = [[plane_tile(target, 0, number, (0, 1))], [plane_tile(target, 1, number, (1,))]]
+            rows = merged_rows(tree, LANES + g * LANE_ROWS * LANE_ROWS + k, LANE_ROWS, True)
+            save_series(series, base + 2 * number * LANE_ROWS, rows)
 
 
 def plane_tile(target, plane, k, parts):
@@ -979,12 +988,13 @@
     return result
 
 
-def unpermuted(columns, out_ref, offset, repeat_bits):
+def unpermuted(columns, out_ref, offset, repeat_bits, bits):
     lane = lane_index((LANE_ROWS, LANES))
     for number in range(len(columns) << repeat_bits):
         row = (lane + number * LANES) >> repeat_bits
         row = row & (LANES - 1)
-        picks = (row & 64) + (row & 7) * LANE_ROWS + ((row >> 3) & 7)
+        block = LANE_ROWS << bits
+        picks = (row & (LANES - block)) + (row & ((1 << bits) - 1)) * LANE_ROWS + ((row & (block - 1)) >> bits)
         column = columns[number >> repeat_bits]
         spread = jnp.take_along_axis(column, picks, axis=1, mode="promise_in_bounds")
         at = offset + number * LANES

time: 21.3 us -> 16.9 us (0.79)
  Pallas kernels: 19.8 us -> 16.1 us
  local copies, waits for them, and re-layouts: 1.28 us -> 0.6 us
    pallas_call x1, Pallas kernels: 19.8 us -> 16.1 us  [search(): pl.pallas_call(search_kernel, in_specs=[pl.BlockSpec(memory_space=pl.ANY)...]
    unnamed x1, local copies, waits for them, and re-layouts: 1.28 us -> 0.6 us
where the time goes in v4:
time: 16.9 us; the launch traced here: 16.8 us
  Pallas kernels  16.1 us (95%)
  local copies, waits for them, and re-layouts  0.6 us (4%)
    pallas_call x1, Pallas kernels, search(): pl.pallas_call(search_kernel, in_specs=[pl.BlockSpec(memory_space=pl.ANY)...  16.1 us
    unnamed x1, local copies, waits for them, and re-layouts  0.6 us

profile of v4, /device:TPU:0, one launch (start us, length us, event | category | flops | bytes accessed | tf_op | source)
XLA Modules:
  0.0 16.8 jit_solution(6103289835747216866)
XLA Ops:
  0.0 16.1 %shard_map.37 = f32[1,1024]{1,0:T(1,128)S(1)} custom-call(bf16[8,512,256]{2,1,0:T(8,128)(2,1)} %x_hbm.1, s32[1,4096]{1,0:T(1,128)} %bitcast.1, s32[9]{0:T(128)} %widths_hbm.1), custom_call_target="tpu_custom_call" | custom-call | tf_op jit(solution)/shard_map/pallas_call | solution.py:731
  16.2 0.6 %copy.5 = f32[1,1024]{1,0:T(1,128)} copy(f32[1,1024]{1,0:T(1,128)S(1)} %shard_map.37) | data formatting | bytes 8192

commit v5 on v4

--- a/solution.py
+++ b/solution.py
@@ -382,7 +382,7 @@
 
 
 def block_span(block):
-    return ((0, 8), (2, 8), (3, 6), (3, 6))[block]
+    return ((0, 4), (0, 4), (1, 4), (1, 4))[block]
 
 
 def late_span(place, whole):
@@ -418,18 +418,17 @@
 
 
 def near_leaves(tiles):
-    if len(tiles) == 4:
-        wide = [plus(tiles[0], tiles[2]), plus(tiles[1], tiles[3])]
-    else:
-        wide = tiles
-    zero = plus(wide[0], wide[1])
-    first = plus(wide[0], stepped(wide[1], 1))
-    message = [None, None, first[0], first[1], zero[0], zero[1], None, None]
-    if len(tiles) == 4:
-        second = [plus(tiles[a], stepped(tiles[2 + a], 1)) for a in range(2)]
-        message[0], message[1] = second[0][0], second[1][0]
-        message[6], message[7] = second[0][1], second[1][1]
-    return message
+    wide = [plus(tiles[0], tiles[2]), plus(tiles[1], tiles[3])] if len(tiles) == 4 else tiles
+    return plus_late(wide) + plus(wide[0], wide[1])
+
+
+def plus_late(pair):
+    return plus(pair[0], stepped(pair[1], 1))
+
+
+def double_leaves(tiles):
+    pairs = [plus_late([tiles[a], tiles[2 + a]]) for a in range(2)]
+    return [pair[part] for part in range(2) for pair in pairs]
 
 
 def far_leaves(tiles):
@@ -445,7 +444,7 @@
 
 def search_kernel(
     x_hbm, mask_hbm, widths_hbm, out_ref, x_ref, unit_ref, mask_ref, widths_ref, in_sem, send, send_sem, recv, recv_sem,
-    ready_sem, first, work, mid, planes, double, lower, series, prefix,
+    twice, twice_sem, taken, taken_sem, peaks, answered, answer_sem, ready_sem, far, far_sem, relay, relay_sem, onward_sem, first, work, mid, planes, double, lower, series, prefix,
 ):
     beams, width, samples = x_ref.shape
     blocks, groups = lax.axis_size("freq"), lax.axis_size("beam")
@@ -472,29 +471,33 @@
         load.start()
     widths_load.start()
 
-    def signal(semaphore, place):
+    def signal(semaphore, block, group):
         pl.semaphore_signal(
-            semaphore, inc=1, device_id={"freq": place // groups, "beam": place % groups},
-            device_id_type=pl.DeviceIdType.MESH,
+            semaphore, inc=1, device_id={"freq": block, "beam": group}, device_id_type=pl.DeviceIdType.MESH,
         )
 
     barrier = pltpu.get_barrier_semaphore()
 
     @pl.when(my_block == 0)
     def _():
-        for step in range(1, devices):
-            signal(barrier, (my_place + devices - step) % devices)
+        for block in (3, 1, 2):
+            for group in range(groups):
+                signal(barrier, block, group)
+        for step in range(1, groups):
+            signal(barrier, 0, (my_group + step) % groups)
 
     @pl.when(my_block == 1)
     def _():
-        for place in range(groups):
-            signal(barrier, place)
+        for group in range(groups):
+            signal(barrier, 0, group)
+        for step in range(1, groups):
+            signal(barrier, 1, (my_group + step) % groups)
 
     @pl.when(my_block >= 2)
     def _():
         pl.semaphore_wait(barrier, groups)
-        for place in range(quarter):
-            signal(ready_sem, place)
+        for group in range(groups):
+            signal(ready_sem, 0, group)
 
     for column in range(prefix.shape[0]):
         prefix[column, :LANE_ROWS] = jnp.zeros((LANE_ROWS, LANES), jnp.float32)
@@ -538,19 +541,18 @@
 
     def summing(depth):
         chosen = band_mask(depth, width)
+        count = chosen.shape[0]
         matrix = jnp.concatenate(
-            [jnp.where(chosen, coarse, 0.0), jnp.where(chosen, fine, 0.0)], axis=1
+            [jnp.where(chosen, coarse, 0.0), jnp.where(chosen, fine, 0.0)], axis=0
         ).astype(jnp.bfloat16)
         shift = jnp.sum(jnp.where(chosen, offset, 0.0), axis=1, keepdims=True)
 
         def tiles(slot):
-            rows = x_ref[(my_group + slot) % beams]
-            sums = jnp.dot(
-                matrix, jnp.concatenate([rows, rows], axis=0), preferred_element_type=jnp.float32
-            ) - shift
+            both = jnp.dot(matrix, x_ref[(my_group + slot) % beams], preferred_element_type=jnp.float32)
+            sums = both[:count] + both[count:] - shift
             return [
                 [sums[t:t + LANE_ROWS, p * LANES:(p + 1) * LANES] for p in range(2)]
-                for t in range(0, chosen.shape[0], LANE_ROWS)
+                for t in range(0, count, LANE_ROWS)
             ]
 
         return tiles
@@ -570,41 +572,97 @@
             action(message(0, slot, *block_span(2)))
             return
 
-        @pl.when(my_block == 1)
+        @pl.when((my_block == 1) | (slot > 0))
         def _():
-            action(message(0, slot, *block_span(1)))
+            action(message(0, slot, *block_span(0)))
+
+    def double_messages(action, slot):
+        def message(begin):
+            return pltpu.make_async_remote_copy(
+                src_ref=twice.at[slot, pl.ds(begin, 4 - begin)],
+                dst_ref=taken.at[my_place, pl.ds(begin, 4 - begin)],
+                send_sem=twice_sem.at[slot],
+                recv_sem=taken_sem.at[my_place],
+                device_id={"freq": 1, "beam": (my_group + slot) % beams},
+                device_id_type=pl.DeviceIdType.MESH,
+            )
+
+        @pl.when(my_block == 0)
+        def _():
+            action(message(0))
         if slot > 0:
-            @pl.when(my_block == 0)
+            @pl.when(my_block == 1)
             def _():
-                action(message(0, slot, *block_span(0)))
-
-    def near_phase(narrow):
+                action(message(2))
+
+    def answer():
+        return pltpu.make_async_remote_copy(
+            src_ref=peaks, dst_ref=answered, send_sem=answer_sem.at[0], recv_sem=answer_sem.at[1],
+            device_id={"freq": 0, "beam": my_group}, device_id_type=pl.DeviceIdType.MESH,
+        )
+
+    def near_phase(narrow, begin, end):
         tiles = summing(0 if narrow else 1)
         batch = 4
-        for begin in range(0, beams, batch):
-            slots = range(begin, begin + batch)
+        for start in range(begin, end, batch):
+            slots = range(start, start + batch)
             for slot, summed in [(slot, tiles(slot)) for slot in slots]:
                 for number, leaf in enumerate(near_leaves(summed)):
-                    if leaf is not None:
+                    if not narrow or number > 0:
                         send[0, slot, number] = leaf.astype(jnp.bfloat16)
+                if not narrow:
+                    for number, leaf in enumerate(double_leaves(summed)):
+                        twice[slot, number] = leaf.astype(jnp.bfloat16)
                 if slot == 0 and not narrow:
                     @pl.when(my_block == 0)
                     def _():
-                        recv[my_place] = send[0, 0]
-            if begin == 0 and not narrow:
-                pl.semaphore_wait(barrier, jnp.where(my_block == 0, 2 * groups - 1, groups))
-            for slot in slots:
-                near_messages(lambda copy: copy.start(), slot, narrow)
+                        recv[my_place, :4] = send[0, 0, :4]
+
+                    @pl.when(my_block == 1)
+                    def _():
+                        taken[my_place] = twice[0]
+            if narrow:
+                for slot in slots:
+                    near_messages(lambda copy: copy.start(), slot, narrow)
 
     def next_messages(action, slot, low):
         action(message(1, slot, 0 if low else 4, 8))
 
-    def last_messages(action, slot):
+    def by_half(source, action):
         for half in range(2):
-            @pl.when((my_group * 2 >= quarter) if half else (my_group * 2 < quarter))
+            @pl.when((source * 2 >= quarter) if half else (source * 2 < quarter))
             def _(half=half):
-                for block in (3, 2):
-                    action(message(block, slot, 4 * half, 8))
+                action(4 * half)
+
+    def passed(row, begin):
+        return pltpu.make_async_remote_copy(
+            src_ref=far.at[quarter + row, :, pl.ds(begin, 8 - begin)],
+            dst_ref=relay.at[row, :, pl.ds(begin, 8 - begin)],
+            send_sem=far_sem.at[quarter + row, 0],
+            recv_sem=relay_sem.at[row],
+            device_id={"freq": 0, "beam": (my_group + quarter) % groups},
+            device_id_type=pl.DeviceIdType.MESH,
+        )
+
+    def direct(beam, block, begin):
+        return pltpu.make_async_remote_copy(
+            src_ref=far.at[beam, block - 2, pl.ds(begin, 8 - begin)],
+            dst_ref=recv.at[my_place, pl.ds(begin, 8 - begin)],
+            send_sem=far_sem.at[beam, block - 2],
+            recv_sem=recv_sem.at[my_place],
+            device_id={"freq": block, "beam": beam},
+            device_id_type=pl.DeviceIdType.MESH,
+        )
+
+    def onward(row, block, begin):
+        return pltpu.make_async_remote_copy(
+            src_ref=relay.at[row, block - 2, pl.ds(begin, 8 - begin)],
+            dst_ref=recv.at[my_place - quarter, pl.ds(begin, 8 - begin)],
+            send_sem=onward_sem.at[row, block - 2],
+            recv_sem=recv_sem.at[my_place - quarter],
+            device_id={"freq": block, "beam": quarter + row},
+            device_id_type=pl.DeviceIdType.MESH,
+        )
 
     def far_phase(low):
         tiles = summing(3 if low else 2)
@@ -614,20 +672,22 @@
             for slot, summed in [(slot, tiles(slot)) for slot in slots]:
                 for block, leaves in far_leaves(summed).items():
                     for number, leaf in enumerate(leaves):
-                        send[block, slot, number] = leaf.astype(jnp.bfloat16)
-            for slot in slots:
-                next_messages(lambda copy: copy.start(), slot, low)
-        if low:
-            pl.semaphore_wait(ready_sem, 2 * groups)
-            for slot in range(beams):
-                last_messages(lambda copy: copy.start(), slot)
-
-    def arrival(place, begin, end):
-        target = recv.at[place, pl.ds(begin, end - begin)]
+                        if block == 1:
+                            send[block, slot, number] = leaf.astype(jnp.bfloat16)
+                        else:
+                            far[(my_group + slot) % beams, block - 2, number] = leaf.astype(jnp.bfloat16)
+            if not low:
+                for slot in slots:
+                    next_messages(lambda copy: copy.start(), slot, low)
+
+    def landed(target, semaphore):
         pltpu.make_async_remote_copy(
-            src_ref=target, dst_ref=target, send_sem=send_sem.at[0, 0], recv_sem=recv_sem.at[place],
+            src_ref=target, dst_ref=target, send_sem=send_sem.at[0, 0], recv_sem=semaphore,
             device_id={"freq": my_block, "beam": my_group}, device_id_type=pl.DeviceIdType.MESH,
         ).wait_recv()
+
+    def arrival(place, begin, end):
+        landed(recv.at[place, pl.ds(begin, end - begin)], recv_sem.at[place])
 
     args = (recv, first, work, mid, series)
     pitch = first.shape[1] // LANE_ROWS
@@ -641,16 +701,31 @@
 
     @pl.when(my_block < 2)
     def _():
-        near_phase(False)
+        near_phase(False, 0, beams)
+
+        @pl.when((my_block == 0) & (my_group < quarter))
+        def _():
+            far_phase(True)
+
+        pl.semaphore_wait(barrier, 2 * groups - 1)
+        for slot in range(beams):
+            near_messages(lambda copy: copy.start(), slot, False)
+        for slot in range(beams):
+            double_messages(lambda copy: copy.start(), slot)
+
+        @pl.when((my_block == 0) & (my_group < quarter))
+        def _():
+            by_half(my_group, lambda begin: [passed(row, begin).start() for row in range(quarter)])
+            for slot in range(beams):
+                next_messages(lambda copy: copy.start(), slot, True)
+
+        @pl.when((my_block == 0) & (my_group >= quarter))
+        def _():
+            far_phase(False)
 
     @pl.when(my_block >= 2)
     def _():
-        near_phase(True)
-
-    for low in (True, False):
-        @pl.when((my_block == 0) & ((my_group < quarter) == low))
-        def _(low=low):
-            far_phase(low)
+        near_phase(True, 0, beams)
 
     widths_load.wait()
 
@@ -660,32 +735,61 @@
             @pl.when(place != my_group)
             def _(place=place):
                 arrival(place, *block_span(0))
-        plane_rows(recv, first, mid, double, 0, groups, 1, ((0, 6), (1, 7)))
         for root in range(2):
-            plane_rows(recv, first, mid, planes.at[root], 0, groups, root, ((4 - 2 * root, 5 - 2 * root),))
+            plane_rows(recv, first, mid, planes.at[root], 0, groups, root, ((2 - 2 * root, 3 - 2 * root),))
+
+        pl.semaphore_wait(ready_sem, 2 * groups)
+
+        @pl.when(my_group < quarter)
+        def _():
+            by_half(my_group, lambda begin: [
+                direct(beam, block, begin).start() for beam in range(quarter) for block in (3, 2)
+            ])
+
+        @pl.when(my_group >= quarter)
+        def _():
+            def pass_on(begin):
+                for row in range(quarter):
+                    landed(relay.at[row, :, pl.ds(begin, 8 - begin)], relay_sem.at[row])
+                    for block in (3, 2):
+                        onward(row, block, begin).start()
+
+            by_half(my_group - quarter, pass_on)
+
         for place in range(groups, 2 * groups):
             arrival(place, *block_span(1))
-        plane_rows(recv, first, mid, double, 1, groups, 1, ((None, 6), (None, 7)))
-        double_rows(double, series, 0)
         for root in range(2):
-            plane_rows(recv, first, mid, planes.at[root], 1, groups, root, ((4 - 2 * root, 5 - 2 * root),))
+            plane_rows(recv, first, mid, planes.at[root], 1, groups, root, ((2 - 2 * root, 3 - 2 * root),))
         for root in range(2):
             lower_rows(planes.at[root], lower.at[root], root)
-        unpermuted(boxcar_rows(widths_ref, series, prefix, 0, 2), out_ref, 512, 1, 4)
         for plane in range(2, blocks):
             for place in range(plane * groups, (plane + 1) * groups):
                 arrival(place, *block_span(2))
             for root in range(2):
-                numbers = ((4, 5) if root == 0 else (None, 3),)
+                numbers = ((2, 3) if root == 0 else (None, 1),)
                 plane_rows(recv, first, mid, planes.at[root], plane, groups, root, numbers)
         for root in range(2):
             upper_rows(planes.at[root], lower.at[root], series, 256 * (1 + root), root)
         result = boxcar_rows(widths_ref, series, prefix, 2, 4)
         unfolded(result[:2], out_ref, 0)
         unfolded(result[2:], out_ref, 256)
+        landed(answered, answer_sem.at[1])
+        unpermuted([answered[column] for column in range(2)], out_ref, 512, 1, 4)
 
     @pl.when(my_block == 1)
     def _():
+        for place in range(groups):
+            landed(taken.at[place], taken_sem.at[place])
+        plane_rows(taken, first, mid, double, 0, groups, 1, ((0, 2), (1, 3)))
+        for place in range(groups, 2 * groups):
+            @pl.when(place != my_place)
+            def _(place=place):
+                landed(taken.at[place, pl.ds(2, 2)], taken_sem.at[place])
+        plane_rows(taken, first, mid, double, 1, groups, 1, ((None, 2), (None, 3)))
+        double_rows(double, series, 256)
+        for number, column in enumerate(boxcar_rows(widths_ref, series, prefix, 2, 2)):
+            peaks[number] = column
+        answer().start()
         for place in range(groups):
             arrival(place, *late_span(place, quarter))
         unit_rows(*args, 0, 1, 256, 2, wide_places(
@@ -695,6 +799,7 @@
             ],
         ))
         unpermuted(boxcar_rows(widths_ref, series, prefix, 0, 2), out_ref, 0, 2, 3)
+        answer().wait_send()
 
     for late in (2, 3):
         @pl.when(my_block == late)
@@ -715,12 +820,25 @@
             @pl.when((my_block >= 2) == narrow)
             def _(narrow=narrow, slot=slot):
                 near_messages(lambda copy: copy.wait_send(), slot, narrow)
+                if not narrow:
+                    double_messages(lambda copy: copy.wait_send(), slot)
         for low in (True, False):
             @pl.when((my_block == 0) & ((my_group < quarter) == low))
             def _(low=low, slot=slot):
                 next_messages(lambda copy: copy.wait_send(), slot, low)
-                if low:
-                    last_messages(lambda copy: copy.wait_send(), slot)
+
+    @pl.when((my_block == 0) & (my_group < quarter))
+    def _():
+        by_half(my_group, lambda begin: [passed(row, begin).wait_send() for row in range(quarter)])
+        by_half(my_group, lambda begin: [
+            direct(beam, block, begin).wait_send() for beam in range(quarter) for block in (3, 2)
+        ])
+
+    @pl.when((my_block == 0) & (my_group >= quarter))
+    def _():
+        by_half(my_group - quarter, lambda begin: [
+            onward(row, block, begin).wait_send() for row in range(quarter) for block in (3, 2)
+        ])
 
 
 def search(intensity, channel_mask, box_widths):
@@ -738,11 +856,23 @@
             pltpu.VMEM((1, width * groups), jnp.int32),
             pltpu.SMEM(box_widths.shape, jnp.int32),
             pltpu.SemaphoreType.DMA((6,)),
-            pltpu.VMEM((blocks, beams, 8, LANE_ROWS, LANES), jnp.bfloat16),
-            pltpu.SemaphoreType.DMA((blocks, beams)),
+            pltpu.VMEM((2, beams, 8, LANE_ROWS, LANES), jnp.bfloat16),
+            pltpu.SemaphoreType.DMA((2, beams)),
             pltpu.VMEM((devices, 8, LANE_ROWS, LANES), jnp.bfloat16),
             pltpu.SemaphoreType.DMA((devices,)),
+            pltpu.VMEM((beams, 4, LANE_ROWS, LANES), jnp.bfloat16),
+            pltpu.SemaphoreType.DMA((beams,)),
+            pltpu.VMEM((2 * groups, 4, LANE_ROWS, LANES), jnp.bfloat16),
+            pltpu.SemaphoreType.DMA((2 * groups,)),
+            pltpu.VMEM((2, LANE_ROWS, LANES), jnp.float32),
+            pltpu.VMEM((2, LANE_ROWS, LANES), jnp.float32),
+            pltpu.SemaphoreType.DMA((2,)),
             pltpu.SemaphoreType.REGULAR,
+            pltpu.VMEM((beams, 2, 8, LANE_ROWS, LANES), jnp.bfloat16),
+            pltpu.SemaphoreType.DMA((beams, 2)),
+            pltpu.VMEM((groups // 2, 2, 8, LANE_ROWS, LANES), jnp.bfloat16),
+            pltpu.SemaphoreType.DMA((groups // 2,)),
+            pltpu.SemaphoreType.DMA((groups // 2, 2)),
             pltpu.VMEM((2, samples + LANE_ROWS * LANE_ROWS, LANES), jnp.float32),
             pltpu.VMEM((2, samples, LANES), jnp.float32),
             pltpu.VMEM((2, samples, LANES), jnp.float32),
@@ -865,18 +995,19 @@
 
 def plane_rows(recv, first, mid, target, plane, groups, root, numbers):
     kinds = len(numbers)
+    origin = (2 * (kinds - 1) + root * (2 - kinds)) * LANE_ROWS * LANE_ROWS
     parts = [part for part in range(2) if numbers[0][part] is not None]
     flat = LANE_ROWS * LANE_ROWS
     for place in range(groups):
         for kind in range(kinds):
             for part in parts:
-                at = kind * flat + place * LANE_ROWS
+                at = origin + kind * flat + place * LANE_ROWS
                 first[part, at:at + LANE_ROWS] = recv[plane * groups + place, numbers[kind][part]].astype(jnp.float32)
 
     def pair_at(source, start):
         return [source[part, pl.ds(start, LANE_ROWS, stride=LANE_ROWS)] if part in parts else None for part in range(2)]
 
-    tree = [[pair_at(first, (tile % kinds) * flat + tile // kinds)] for tile in range(kinds * LANE_ROWS)]
+    tree = [[pair_at(first, origin + (tile % kinds) * flat + tile // kinds)] for tile in range(kinds * LANE_ROWS)]
     level_root = root
     while len(tree) > 1:
         tree = [
@@ -889,9 +1020,10 @@
         level_root = level_root * 2
     for j, pair in enumerate(tree[0]):
         for part in parts:
-            mid[part, j * LANE_ROWS:(j + 1) * LANE_ROWS] = pair[part]
+            at = origin + j * LANE_ROWS
+            mid[part, at:at + LANE_ROWS] = pair[part]
     for g in range(kinds):
-        tree = [[pair_at(mid, g * flat + p)] for p in range(LANE_ROWS)]
+        tree = [[pair_at(mid, origin + g * flat + p)] for p in range(LANE_ROWS)]
         for k, pair in enumerate(merged_rows(tree, (root * kinds + g) * LANE_ROWS, 1, False)):
             at = g * flat + k * LANE_ROWS
             for part in parts:

time: 16.9 us -> 15.9 us (0.941)
  Pallas kernels: 16.1 us -> 15.2 us
    pallas_call x1, Pallas kernels: 16.1 us -> 15.2 us  [search(): pl.pallas_call(search_kernel, in_specs=[pl.BlockSpec(memory_space=pl.ANY)...]
where the time goes in v5:
time: 15.9 us; the launch traced here: 15.8 us
  Pallas kernels  15.2 us (96%)
  local copies, waits for them, and re-layouts  0.6 us (4%)
    pallas_call x1, Pallas kernels, search(): pl.pallas_call(search_kernel, in_specs=[pl.BlockSpec(memory_space=pl.ANY)...  15.2 us
    unnamed x1, local copies, waits for them, and re-layouts  0.6 us

profile of v5, /device:TPU:0, one launch (start us, length us, event | category | flops | bytes accessed | tf_op | source)
XLA Modules:
  0.0 15.8 jit_solution(1285528166547283577)
XLA Ops:
  0.0 15.2 %shard_map.37 = f32[1,1024]{1,0:T(1,128)S(1)} custom-call(bf16[8,512,256]{2,1,0:T(8,128)(2,1)} %x_hbm.1, s32[1,4096]{1,0:T(1,128)} %bitcast.1, s32[9]{0:T(128)} %widths_hbm.1), custom_call_target="tpu_custom_call" | custom-call | tf_op jit(solution)/shard_map/pallas_call | solution.py:849
  15.2 0.6 %copy.5 = f32[1,1024]{1,0:T(1,128)} copy(f32[1,1024]{1,0:T(1,128)S(1)} %shard_map.37) | data formatting | bytes 8192

commit v6 on v5

--- a/solution.py
+++ b/solution.py
@@ -735,8 +735,8 @@
             @pl.when(place != my_group)
             def _(place=place):
                 arrival(place, *block_span(0))
-        for root in range(2):
-            plane_rows(recv, first, mid, planes.at[root], 0, groups, root, ((2 - 2 * root, 3 - 2 * root),))
+        both = ((2, 3), (0, 1))
+        plane_rows(recv, first, mid, groups, [(planes.at[root], 0, root, (both[root],)) for root in range(2)])
 
         pl.semaphore_wait(ready_sem, 2 * groups)
 
@@ -758,18 +758,16 @@
 
         for place in range(groups, 2 * groups):
             arrival(place, *block_span(1))
-        for root in range(2):
-            plane_rows(recv, first, mid, planes.at[root], 1, groups, root, ((2 - 2 * root, 3 - 2 * root),))
-        for root in range(2):
-            lower_rows(planes.at[root], lower.at[root], root)
+        plane_rows(recv, first, mid, groups, [(planes.at[root], 1, root, (both[root],)) for root in range(2)])
+        lower_rows(planes, lower)
+        late = ((2, 3), (None, 1))
         for plane in range(2, blocks):
             for place in range(plane * groups, (plane + 1) * groups):
                 arrival(place, *block_span(2))
-            for root in range(2):
-                numbers = ((2, 3) if root == 0 else (None, 1),)
-                plane_rows(recv, first, mid, planes.at[root], plane, groups, root, numbers)
-        for root in range(2):
-            upper_rows(planes.at[root], lower.at[root], series, 256 * (1 + root), root)
+        plane_rows(recv, first, mid, groups, [
+            (planes.at[root], plane, root, (late[root],)) for plane in range(2, blocks) for root in range(2)
+        ])
+        upper_rows(planes, lower, series)
         result = boxcar_rows(widths_ref, series, prefix, 2, 4)
         unfolded(result[:2], out_ref, 0)
         unfolded(result[2:], out_ref, 256)
@@ -780,12 +778,12 @@
     def _():
         for place in range(groups):
             landed(taken.at[place], taken_sem.at[place])
-        plane_rows(taken, first, mid, double, 0, groups, 1, ((0, 2), (1, 3)))
+        plane_rows(taken, first, mid, groups, [(double, 0, 1, ((0, 2), (1, 3)))])
         for place in range(groups, 2 * groups):
             @pl.when(place != my_place)
             def _(place=place):
                 landed(taken.at[place, pl.ds(2, 2)], taken_sem.at[place])
-        plane_rows(taken, first, mid, double, 1, groups, 1, ((None, 2), (None, 3)))
+        plane_rows(taken, first, mid, groups, [(double, 1, 1, ((None, 2), (None, 3)))])
         double_rows(double, series, 256)
         for number, column in enumerate(boxcar_rows(widths_ref, series, prefix, 2, 2)):
             peaks[number] = column
@@ -889,17 +887,21 @@
 
 def ramped(pair, start, stride, far, only_late=False):
     shape = pair[1].shape
-    place = lane_index(shape) + (lax.broadcasted_iota(jnp.int32, shape, 0) * stride + start)
-    picks = place & (LANES - 1)
-    late = jnp.take_along_axis(pair[1], picks, axis=1, mode="promise_in_bounds")
+    reach = (LANE_ROWS - 1) * stride
+    place = lane_index(shape) + (start + reach - lax.broadcasted_iota(jnp.int32, shape, 0) * stride)
+    turn = (-start - reach) % LANES
+
+    def turned(piece):
+        if turn + reach < LANES:
+            return pltpu.roll(piece, turn, 1, stride=stride, stride_axis=0)
+        return jnp.take_along_axis(piece, place & (LANES - 1), axis=1, mode="promise_in_bounds")
+
+    late = turned(pair[1])
     if far:
         return [jnp.where(place < 2 * LANES, late, 0.0), None]
     near = place < LANES
-    moved = [None, jnp.where(near, late, 0.0)]
-    if not only_late:
-        early = jnp.take_along_axis(pair[0], picks, axis=1, mode="promise_in_bounds")
-        moved[0] = jnp.where(near, early, late)
-    return moved
+    early = None if only_late else jnp.where(near, turned(pair[0]), late)
+    return [early, jnp.where(near, late, 0.0)]
 
 
 def joined_pair(low, high):
@@ -957,7 +959,7 @@
             level_root = level_root * 2
         for k in range(chunks):
             for part in range(2):
-                at = (j * chunks + k) * LANE_ROWS
+                at = (j * chunks + k ^ LANE_ROWS - 1) * LANE_ROWS
                 mid[part, at:at + LANE_ROWS] = tree[0][k][part]
     far = root > 0
     for g in range(tiles // LANE_ROWS):
@@ -993,41 +995,51 @@
     return tree[0]
 
 
-def plane_rows(recv, first, mid, target, plane, groups, root, numbers):
-    kinds = len(numbers)
-    origin = (2 * (kinds - 1) + root * (2 - kinds)) * LANE_ROWS * LANE_ROWS
-    parts = [part for part in range(2) if numbers[0][part] is not None]
+def plane_rows(recv, first, mid, groups, jobs):
     flat = LANE_ROWS * LANE_ROWS
-    for place in range(groups):
-        for kind in range(kinds):
+    origins, origin = [], 0
+    for target, plane, root, numbers in jobs:
+        origins.append(origin)
+        origin += len(numbers) * flat
+    used = [[part for part in range(2) if numbers[0][part] is not None] for _, _, _, numbers in jobs]
+    for (target, plane, root, numbers), origin, parts in zip(jobs, origins, used):
+        for place in range(groups):
+            for kind in range(len(numbers)):
+                for part in parts:
+                    at = origin + kind * flat + place * LANE_ROWS
+                    rows = recv[plane * groups + place, numbers[kind][part]]
+                    first[part, at:at + LANE_ROWS] = rows.astype(jnp.float32)
+
+    def pair_at(source, parts, start):
+        return [source[part, pl.ds(start, LANE_ROWS, stride=LANE_ROWS)] if part in parts else None for part in range(2)]
+
+    for (target, plane, root, numbers), origin, parts in zip(jobs, origins, used):
+        kinds = len(numbers)
+        tree = [
+            [pair_at(first, parts, origin + (tile % kinds) * flat + tile // kinds)]
+            for tile in range(kinds * LANE_ROWS)
+        ]
+        level_root = root
+        while len(tree) > 1:
+            tree = [
+                [
+                    joined_pair(low[r // 2], stepped(high[r // 2], level_root + r // 2 + r % 2))
+                    for r in range(2 * len(low))
+                ]
+                for low, high in zip(tree[0::2], tree[1::2])
+            ]
+            level_root = level_root * 2
+        for j, pair in enumerate(tree[0]):
             for part in parts:
-                at = origin + kind * flat + place * LANE_ROWS
-                first[part, at:at + LANE_ROWS] = recv[plane * groups + place, numbers[kind][part]].astype(jnp.float32)
-
-    def pair_at(source, start):
-        return [source[part, pl.ds(start, LANE_ROWS, stride=LANE_ROWS)] if part in parts else None for part in range(2)]
-
-    tree = [[pair_at(first, origin + (tile % kinds) * flat + tile // kinds)] for tile in range(kinds * LANE_ROWS)]
-    level_root = root
-    while len(tree) > 1:
-        tree = [
-            [
-                joined_pair(low[r // 2], stepped(high[r // 2], level_root + r // 2 + r % 2))
-                for r in range(2 * len(low))
-            ]
-            for low, high in zip(tree[0::2], tree[1::2])
-        ]
-        level_root = level_root * 2
-    for j, pair in enumerate(tree[0]):
-        for part in parts:
-            at = origin + j * LANE_ROWS
-            mid[part, at:at + LANE_ROWS] = pair[part]
-    for g in range(kinds):
-        tree = [[pair_at(mid, origin + g * flat + p)] for p in range(LANE_ROWS)]
-        for k, pair in enumerate(merged_rows(tree, (root * kinds + g) * LANE_ROWS, 1, False)):
-            at = g * flat + k * LANE_ROWS
-            for part in parts:
-                target[plane, part, at:at + LANE_ROWS] = pair[part]
+                at = origin + (j ^ LANE_ROWS - 1) * LANE_ROWS
+                mid[part, at:at + LANE_ROWS] = pair[part]
+    for (target, plane, root, numbers), origin, parts in zip(jobs, origins, used):
+        for g in range(len(numbers)):
+            tree = [[pair_at(mid, parts, origin + g * flat + p)] for p in range(LANE_ROWS)]
+            for k, pair in enumerate(merged_rows(tree, (root * len(numbers) + g) * LANE_ROWS, 1, False)):
+                at = g * flat + k * LANE_ROWS
+                for part in parts:
+                    target[plane, part, at:at + LANE_ROWS] = pair[part]
 
 
 def double_rows(target, series, base):
@@ -1045,27 +1057,31 @@
     ]
 
 
-def lower_rows(target, lower, root):
+def lower_rows(planes, lower):
     for k in range(LANE_ROWS):
-        tree = [[plane_tile(target, plane, k, (0, 1))] for plane in range(2)]
-        for q, pair in enumerate(merged_rows(tree, root * LANE_ROWS * LANE_ROWS + k, LANE_ROWS, False)):
-            for part in range(2):
+        for root in range(2):
+            tree = [[plane_tile(planes.at[root], plane, k, (0, 1))] for plane in range(2)]
+            for q, pair in enumerate(merged_rows(tree, root * LANE_ROWS * LANE_ROWS + k, LANE_ROWS, False)):
+                for part in range(2):
+                    at = (2 * k + q) * LANE_ROWS
+                    lower[root, part, at:at + LANE_ROWS] = pair[part]
+
+
+def upper_rows(planes, lower, series):
+    for root in range(2):
+        parts = (0, 1) if root == 0 else (1,)
+        for k in range(LANE_ROWS):
+            begin = root * LANE_ROWS * LANE_ROWS + k
+            tree = [[plane_tile(planes.at[root], plane, k, parts)] for plane in (2, 3)]
+            high = merged_rows(tree, begin, LANE_ROWS, False)
+            low = []
+            for q in range(2):
                 at = (2 * k + q) * LANE_ROWS
-                lower[part, at:at + LANE_ROWS] = pair[part]
-
-
-def upper_rows(target, lower, series, base, root):
-    parts = (0, 1) if root == 0 else (1,)
-    for k in range(LANE_ROWS):
-        begin = root * LANE_ROWS * LANE_ROWS + k
-        high = merged_rows([[plane_tile(target, plane, k, parts)] for plane in (2, 3)], begin, LANE_ROWS, False)
-        low = []
-        for q in range(2):
-            at = (2 * k + q) * LANE_ROWS
-            low.append([lower[part, at:at + LANE_ROWS] for part in range(2)])
-        rows = merged_rows([low, high], begin * 2, 2 * LANE_ROWS, root > 0)
-        for number in range(0, 4, 2):
-            save_series(series, base + (4 * k + number) * LANE_ROWS, rows[number:number + 2])
+                low.append([lower[root, part, at:at + LANE_ROWS] for part in range(2)])
+            rows = merged_rows([low, high], begin * 2, 2 * LANE_ROWS, root > 0)
+            for number in range(0, 4, 2):
+                at = (32 * (1 + root) + 4 * k + number) * LANE_ROWS
+                save_series(series, at, rows[number:number + 2])
 
 
 def save_series(series, at, pairs):
@@ -1079,7 +1095,7 @@
 def unfolded(columns, out_ref, offset):
     lane = lane_index((LANE_ROWS, LANES))
     for number in range(2):
-        picks = (lane & 15) * LANE_ROWS + (lane >> 5) + 4 * number
+        picks = (lane & 15) * LANE_ROWS + (LANE_ROWS - 1) - (lane >> 5) - 4 * number
         spread = [jnp.take_along_axis(column, picks, axis=1, mode="promise_in_bounds") for column in columns]
         at = offset + number * LANES
         out_ref[:, at:at + LANES] = jnp.where(lane & 16 == 0, spread[0], spread[1])[:1]
@@ -1126,7 +1142,7 @@
         row = (lane + number * LANES) >> repeat_bits
         row = row & (LANES - 1)
         block = LANE_ROWS << bits
-        picks = (row & (LANES - block)) + (row & ((1 << bits) - 1)) * LANE_ROWS + ((row & (block - 1)) >> bits)
+        picks = (row & (LANES - block)) + (row & ((1 << bits) - 1)) * LANE_ROWS + (LANE_ROWS - 1) - ((row & (block - 1)) >> bits)
         column = columns[number >> repeat_bits]
         spread = jnp.take_along_axis(column, picks, axis=1, mode="promise_in_bounds")
         at = offset + number * LANES

time: 15.9 us -> 15.8 us (level)
  no operation moved by 1% of the time
where the time goes in v6:
time: 15.8 us; the launch traced here: 15.7 us
  Pallas kernels  15.1 us (96%)
  local copies, waits for them, and re-layouts  0.6 us (4%)
    pallas_call x1, Pallas kernels, search(): pl.pallas_call(search_kernel, in_specs=[pl.BlockSpec(memory_space=pl.ANY)...  15.1 us
    unnamed x1, local copies, waits for them, and re-layouts  0.6 us

profile of v6, /device:TPU:0, one launch (start us, length us, event | category | flops | bytes accessed | tf_op | source)
XLA Modules:
  0.0 15.7 jit_solution(7415045462036808367)
XLA Ops:
  0.0 15.1 %shard_map.37 = f32[1,1024]{1,0:T(1,128)S(1)} custom-call(bf16[8,512,256]{2,1,0:T(8,128)(2,1)} %x_hbm.1, s32[1,4096]{1,0:T(1,128)} %bitcast.1, s32[9]{0:T(128)} %widths_hbm.1), custom_call_target="tpu_custom_call" | custom-call | tf_op jit(solution)/shard_map/pallas_call | solution.py:847
  15.1 0.6 %copy.5 = f32[1,1024]{1,0:T(1,128)} copy(f32[1,1024]{1,0:T(1,128)S(1)} %shard_map.37) | data formatting | bytes 8192

commit v7 on v6

--- a/solution.py
+++ b/solution.py
@@ -709,9 +709,9 @@
 
         pl.semaphore_wait(barrier, 2 * groups - 1)
         for slot in range(beams):
+            double_messages(lambda copy: copy.start(), slot)
+        for slot in range(beams):
             near_messages(lambda copy: copy.start(), slot, False)
-        for slot in range(beams):
-            double_messages(lambda copy: copy.start(), slot)
 
         @pl.when((my_block == 0) & (my_group < quarter))
         def _():
@@ -764,9 +764,7 @@
         for plane in range(2, blocks):
             for place in range(plane * groups, (plane + 1) * groups):
                 arrival(place, *block_span(2))
-        plane_rows(recv, first, mid, groups, [
-            (planes.at[root], plane, root, (late[root],)) for plane in range(2, blocks) for root in range(2)
-        ])
+            plane_rows(recv, first, mid, groups, [(planes.at[root], plane, root, (late[root],)) for root in range(2)])
         upper_rows(planes, lower, series)
         result = boxcar_rows(widths_ref, series, prefix, 2, 4)
         unfolded(result[:2], out_ref, 0)

time: 15.8 us -> 15.8 us (level)
  no operation moved by 1% of the time
where the time goes in v7:
time: 15.8 us; the launch traced here: 15.6 us
  Pallas kernels  15 us (95%)
  local copies, waits for them, and re-layouts  0.6 us (4%)
    pallas_call x1, Pallas kernels, search(): pl.pallas_call(search_kernel, in_specs=[pl.BlockSpec(memory_space=pl.ANY)...  15 us
    unnamed x1, local copies, waits for them, and re-layouts  0.6 us

profile of v7, /device:TPU:0, one launch (start us, length us, event | category | flops | bytes accessed | tf_op | source)
XLA Modules:
  0.0 15.6 jit_solution(2242710156808936759)
XLA Ops:
  0.0 15.0 %shard_map.37 = f32[1,1024]{1,0:T(1,128)S(1)} custom-call(bf16[8,512,256]{2,1,0:T(8,128)(2,1)} %x_hbm.1, s32[1,4096]{1,0:T(1,128)} %bitcast.1, s32[9]{0:T(128)} %widths_hbm.1), custom_call_target="tpu_custom_call" | custom-call | tf_op jit(solution)/shard_map/pallas_call | solution.py:845
  15.0 0.6 %copy.5 = f32[1,1024]{1,0:T(1,128)} copy(f32[1,1024]{1,0:T(1,128)S(1)} %shard_map.37) | data formatting | bytes 8192

commit v8 on v7

--- a/solution.py
+++ b/solution.py
@@ -774,14 +774,14 @@
 
     @pl.when(my_block == 1)
     def _():
-        for place in range(groups):
-            landed(taken.at[place], taken_sem.at[place])
-        plane_rows(taken, first, mid, groups, [(double, 0, 1, ((0, 2), (1, 3)))])
         for place in range(groups, 2 * groups):
             @pl.when(place != my_place)
             def _(place=place):
                 landed(taken.at[place, pl.ds(2, 2)], taken_sem.at[place])
         plane_rows(taken, first, mid, groups, [(double, 1, 1, ((None, 2), (None, 3)))])
+        for place in range(groups):
+            landed(taken.at[place], taken_sem.at[place])
+        plane_rows(taken, first, mid, groups, [(double, 0, 1, ((0, 2), (1, 3)))])
         double_rows(double, series, 256)
         for number, column in enumerate(boxcar_rows(widths_ref, series, prefix, 2, 2)):
             peaks[number] = column

time: 15.8 us -> 15.8 us (level)
  no operation moved by 1% of the time
where the time goes in v8:
time: 15.8 us; the launch traced here: 15.7 us
  Pallas kernels  15.1 us (96%)
  local copies, waits for them, and re-layouts  0.6 us (4%)
    pallas_call x1, Pallas kernels, search(): pl.pallas_call(search_kernel, in_specs=[pl.BlockSpec(memory_space=pl.ANY)...  15.1 us
    unnamed x1, local copies, waits for them, and re-layouts  0.6 us

profile of v8, /device:TPU:0, one launch (start us, length us, event | category | flops | bytes accessed | tf_op | source)
XLA Modules:
  0.0 15.7 jit_solution(5663757969023470758)
XLA Ops:
  0.0 15.1 %shard_map.37 = f32[1,1024]{1,0:T(1,128)S(1)} custom-call(bf16[8,512,256]{2,1,0:T(8,128)(2,1)} %x_hbm.1, s32[1,4096]{1,0:T(1,128)} %bitcast.1, s32[9]{0:T(128)} %widths_hbm.1), custom_call_target="tpu_custom_call" | custom-call | tf_op jit(solution)/shard_map/pallas_call | solution.py:845
  15.1 0.6 %copy.5 = f32[1,1024]{1,0:T(1,128)} copy(f32[1,1024]{1,0:T(1,128)S(1)} %shard_map.37) | data formatting | bytes 8192
